TPU v7x, 128 devices: a whole 4x4x4 slice. The times are simulated.
128 devices in a mesh: ep: 64 (over z, x, y), tp: 2 (over core).
Axes of the slice: x: 4, y: 4, z: 4, core: 2. Of those that a mesh axis runs over, the one named last changes fastest.
Arguments:
- residual_in: bfloat16 [16384, 2048], P(('ep', 'tp')), may hold values from -24 to 24
- routes: int32 [16384, 8], P('ep'), may hold values from 0 to 63, all different within a row
- segment_ids: int32 [64, 256], P('ep'), may hold values from 0 to 3, never falling along the last dimension, each value on 1 to 128 neighbouring positions
- gain_attn: float32 [2048], replicated, may hold values from 0.5 to 1.5
- w_query: bfloat16 [2048, 2048], P(None, 'tp'), may hold values from -0.125 to 0.125
- w_key: bfloat16 [2048, 2048], P(None, 'tp'), may hold values from -0.125 to 0.125
- w_value: bfloat16 [2048, 2048], P(None, 'tp'), may hold values from -0.125 to 0.125
- gain_query: float32 [16, 128], P('tp'), may hold values from 0.5 to 1.5
- gain_key: float32 [16, 128], P('tp'), may hold values from 0.5 to 1.5
- w_out: bfloat16 [2048, 2048], P('tp'), may hold values from -1 to 1
- gain_moe: float32 [2048], replicated, may hold values from 0.5 to 1.5
- w_router: bfloat16 [2048, 64], replicated, may hold values from -0.25 to 0.25
- w_gate: bfloat16 [64, 2048, 1024], P('ep', None, 'tp'), may hold values from -0.125 to 0.125
- w_up: bfloat16 [64, 2048, 1024], P('ep', None, 'tp'), may hold values from -0.125 to 0.125
- w_down: bfloat16 [64, 1024, 2048], P('ep', 'tp'), may hold values from -1.5 to 1.5
- cotangent: bfloat16 [16384, 2048], P(('ep', 'tp')), may hold values from -24 to 24
Outputs:
- output: bfloat16 [16384, 2048], P(('ep', 'tp'))
- grad_input: float32 [16384, 2048], P(('ep', 'tp'))
- grad_gain_attn: float32 [2048], P(('ep', 'tp'))
- grad_w_query: float32 [2048, 2048], P('ep', 'tp')
- grad_w_key: float32 [2048, 2048], P('ep', 'tp')
- grad_w_value: float32 [2048, 2048], P('ep', 'tp')
- grad_gain_query: float32 [16, 128], P('tp', 'ep')
- grad_gain_key: float32 [16, 128], P('tp', 'ep')
- grad_w_out: float32 [2048, 2048], P('tp', 'ep')
- grad_gain_moe: float32 [2048], P(('ep', 'tp'))
- grad_w_router: float32 [2048, 64], P(('ep', 'tp'))
- grad_w_gate: float32 [64, 2048, 1024], P('ep', None, 'tp')
- grad_w_up: float32 [64, 2048, 1024], P('ep', None, 'tp')
- grad_w_down: float32 [64, 1024, 2048], P('ep', 'tp')
- counts: int32 [64], P('ep')
Inputs may be any that keep to these rules, and one draw needn't show every extreme that they name: `routes`: each token names 8 different experts. `segment_ids`: ids never fall along a row; every row holds 4 documents of at most 128 tokens, one of exactly that many.
All inputs are finite; a program needn't handle non-finite values.
Results may differ from a plain program's by a relative error of at most 0.02.
Values may be sent and summed in bfloat16 or wider, within the bound.
No kernel may reach another device: no remote copies, remote signals or barrier semaphores. Data moves between devices by JAX's collectives and lax.ppermute only.
A program may use at most 256 MiB of HBM per device.

v0:
```python
import jax
import jax.numpy as jnp
from jax import lax
from jax.sharding import PartitionSpec as P

norm_eps = 1e-05
rope_base = 10000.0
mask_fill = -1e30


def rms_scale(values):
    return lax.rsqrt(jnp.mean(values * values, axis=-1, keepdims=True) + norm_eps)


def positions_of(segment_row):
    places = jnp.arange(segment_row.shape[0], dtype=jnp.int32)
    fresh = jnp.concatenate([jnp.ones((1,), dtype=jnp.bool_), segment_row[1:] != segment_row[:-1]])
    starts = jnp.where(fresh, places, jnp.zeros_like(places))
    return places - lax.cummax(starts, axis=0)


def rope_angles(positions, head_dim):
    half_dim = head_dim // 2
    exponent = jnp.arange(half_dim, dtype=jnp.float32) * (2.0 / head_dim)
    inverse = jnp.power(jnp.float32(rope_base), -exponent)
    angles = positions.astype(jnp.float32)[:, None] * inverse[None, :]
    return (jnp.cos(angles), jnp.sin(angles))


def rotate(values, cosine, sine):
    half_dim = values.shape[-1] // 2
    first_half = values[..., :half_dim]
    second_half = values[..., half_dim:]
    cos_b = cosine[:, None, :]
    sin_b = sine[:, None, :]
    return jnp.concatenate(
        [first_half * cos_b - second_half * sin_b, second_half * cos_b + first_half * sin_b],
        axis=-1,
    )


def rotate_back(grads, cosine, sine):
    half_dim = grads.shape[-1] // 2
    first_half = grads[..., :half_dim]
    second_half = grads[..., half_dim:]
    cos_b = cosine[:, None, :]
    sin_b = sine[:, None, :]
    return jnp.concatenate(
        [first_half * cos_b + second_half * sin_b, second_half * cos_b - first_half * sin_b],
        axis=-1,
    )


def slot_tables(route_row, experts, capacity):
    seq_len, top_count = route_row.shape
    route_hits = (
        route_row[:, :, None] == jnp.arange(experts, dtype=jnp.int32)[None, None, :]
    ).astype(jnp.int32)
    per_token = jnp.sum(route_hits, axis=1)
    earlier = jnp.cumsum(per_token, axis=0) - per_token
    rank_ids = jnp.sum(route_hits * earlier[:, None, :], axis=2)
    kept_pair = rank_ids < capacity
    slot_ids = jnp.where(kept_pair, route_row * capacity + rank_ids, experts * capacity)
    owners = jnp.repeat(jnp.arange(seq_len, dtype=jnp.int32), top_count)
    slot_token = (
        jnp.full((experts * capacity + 1,), seq_len, dtype=jnp.int32)
        .at[slot_ids.reshape(-1)]
        .set(owners)
    )
    return (slot_ids, kept_pair, slot_token[: experts * capacity], jnp.sum(per_token, axis=0))


def block_scores(q_block, k_rot, seg_block, seg_row, row_start, block_rows, score_scale):
    places = jnp.arange(seg_row.shape[0], dtype=jnp.int32)
    place_block = row_start + jnp.arange(block_rows, dtype=jnp.int32)
    scores = (
        jnp.einsum("qhd,khd->hqk", q_block, k_rot, preferred_element_type=jnp.float32) * score_scale
    )
    allowed = (seg_block[:, None] == seg_row[None, :]) & (places[None, :] <= place_block[:, None])
    return jnp.where(allowed[None], scores, mask_fill)


def attention_forward(q_rot, k_rot, v_heads, seg_row, block_rows, score_scale):
    seq_len = q_rot.shape[0]

    def one_block(block_id):
        row_start = block_id * block_rows
        scores = block_scores(q_rot, k_rot, seg_row, seg_row, row_start, block_rows, score_scale)
        row_peak = jnp.max(scores, axis=-1, keepdims=True)
        shifted_exp = jnp.exp(scores - row_peak)
        row_total = jnp.sum(shifted_exp, axis=-1, keepdims=True)
        weights = (shifted_exp / row_total).astype(jnp.bfloat16)
        mixed = jnp.einsum("hqk,khd->qhd", weights, v_heads, preferred_element_type=jnp.float32)
        return (mixed, (row_peak + jnp.log(row_total))[..., 0])

    mixed, log_total = lax.map(one_block, jnp.arange(seq_len // block_rows))
    return (mixed.reshape(seq_len, q_rot.shape[1], q_rot.shape[2]), log_total)


def attention_backward(
    q_rot, k_rot, v_heads, grad_mixed, log_total, seg_row, block_rows, score_scale
):
    seq_len = q_rot.shape[0]

    def one_block(carry, block_id):
        grad_keys, grad_values = carry
        row_start = block_id * block_rows
        scores = block_scores(q_rot, k_rot, seg_row, seg_row, row_start, block_rows, score_scale)
        weights = jnp.exp(scores - log_total[block_id][..., None])
        grad_weights = jnp.einsum(
            "qhd,khd->hqk", grad_mixed, v_heads, preferred_element_type=jnp.float32
        )
        inner_sum = jnp.sum(weights * grad_weights, axis=-1, keepdims=True)
        grad_scores = (weights * (grad_weights - inner_sum)).astype(jnp.bfloat16)
        grad_queries = (
            jnp.einsum("hqk,khd->qhd", grad_scores, k_rot, preferred_element_type=jnp.float32)
            * score_scale
        )
        grad_keys = (
            grad_keys
            + jnp.einsum("hqk,qhd->khd", grad_scores, q_rot, preferred_element_type=jnp.float32)
            * score_scale
        )
        grad_values = grad_values + jnp.einsum(
            "hqk,qhd->khd",
            weights.astype(jnp.bfloat16),
            grad_mixed,
            preferred_element_type=jnp.float32,
        )
        return ((grad_keys, grad_values), grad_queries)

    zero_heads = jnp.zeros(k_rot.shape, jnp.float32)
    (grad_keys, grad_values), grad_queries = lax.scan(
        one_block, (zero_heads, zero_heads), jnp.arange(seq_len // block_rows)
    )
    return (grad_queries.reshape(q_rot.shape), grad_keys, grad_values)


def contract_rows(left, right):
    return lax.dot_general(
        left, right, (((0,), (0,)), ((), ())), preferred_element_type=jnp.float32
    )


def contract_cols(left, right):
    return lax.dot_general(
        left, right, (((1,), (1,)), ((), ())), preferred_element_type=jnp.float32
    )


def send_back(slot_grads):
    return lax.all_to_all(slot_grads, "ep", split_axis=0, concat_axis=0, tiled=True)


def local(
    residual_in,
    routes,
    segment_ids,
    gain_attn,
    w_query,
    w_key,
    w_value,
    gain_query,
    gain_key,
    w_out,
    gain_moe,
    w_router,
    w_gate,
    w_up,
    w_down,
    cotangent,
):
    tp_size = lax.axis_size("tp")
    ep_size = lax.axis_size("ep")
    core_index = lax.axis_index("tp")
    own_rows = residual_in.shape[0]
    model_width = residual_in.shape[1]
    local_width = w_query.shape[1]
    local_heads = gain_query.shape[0]
    head_dim = gain_query.shape[1]
    full_width = local_width * tp_size
    local_experts = w_gate.shape[0]
    experts = local_experts * ep_size
    seq_len, top_count = routes.shape
    capacity = seq_len * top_count // experts
    block_rows = min(512, seq_len)
    score_scale = head_dim ** (-0.5)
    seg_row = segment_ids[0]
    first_row = core_index * own_rows
    whole_in = lax.all_gather(residual_in, "tp", axis=0, tiled=True).astype(jnp.float32)
    scale_attn = rms_scale(whole_in)
    normed = (whole_in * scale_attn * gain_attn).astype(jnp.bfloat16)
    queries = jnp.dot(normed, w_query, preferred_element_type=jnp.float32)
    key_proj = jnp.dot(normed, w_key, preferred_element_type=jnp.float32)
    values = jnp.dot(normed, w_value, preferred_element_type=jnp.float32).astype(jnp.bfloat16)
    query_sq, key_sq = lax.psum(
        (jnp.sum(queries * queries, axis=1), jnp.sum(key_proj * key_proj, axis=1)), "tp"
    )
    query_scale = lax.rsqrt(query_sq / full_width + norm_eps)[:, None]
    key_scale = lax.rsqrt(key_sq / full_width + norm_eps)[:, None]
    query_gain = gain_query.reshape(-1)
    key_gain = gain_key.reshape(-1)
    query_unit = queries * query_scale
    key_unit = key_proj * key_scale
    cosine, sine = rope_angles(positions_of(seg_row), head_dim)
    q_rot = rotate(
        (query_unit * query_gain).reshape(seq_len, local_heads, head_dim), cosine, sine
    ).astype(jnp.bfloat16)
    k_rot = rotate(
        (key_unit * key_gain).reshape(seq_len, local_heads, head_dim), cosine, sine
    ).astype(jnp.bfloat16)
    v_heads = values.reshape(seq_len, local_heads, head_dim)
    mixed, log_total = attention_forward(q_rot, k_rot, v_heads, seg_row, block_rows, score_scale)
    mixed_flat = mixed.reshape(seq_len, local_width).astype(jnp.bfloat16)
    branch = lax.psum(jnp.dot(mixed_flat, w_out, preferred_element_type=jnp.float32), "tp")
    hidden_state = whole_in + branch
    scale_moe = rms_scale(hidden_state)
    normed_moe = (hidden_state * scale_moe * gain_moe).astype(jnp.bfloat16)
    logits = jnp.dot(normed_moe, w_router, preferred_element_type=jnp.float32)
    router_probs = jax.nn.softmax(logits, axis=-1)
    slot_ids, kept_pair, slot_token, route_counts = slot_tables(routes, experts, capacity)
    kept_float = kept_pair.astype(jnp.float32)
    pair_weight = jnp.take_along_axis(router_probs, routes, axis=1) * kept_float
    safe_slots = jnp.minimum(slot_ids, experts * capacity - 1)
    zero_row = jnp.zeros((1, model_width), jnp.bfloat16)
    padded_moe = jnp.concatenate([normed_moe, zero_row], axis=0)
    outgoing = padded_moe[slot_token].reshape(experts, capacity, model_width)
    landed = lax.all_to_all(outgoing, "ep", split_axis=0, concat_axis=0, tiled=True)
    width_slots = landed.shape[1]
    grouped = landed.reshape(ep_size, local_experts, width_slots, model_width)
    gate_act = jnp.einsum("secd,edf->secf", grouped, w_gate, preferred_element_type=jnp.float32)
    up_act = jnp.einsum("secd,edf->secf", grouped, w_up, preferred_element_type=jnp.float32)
    inner_act = (gate_act * jax.nn.sigmoid(gate_act) * up_act).astype(jnp.bfloat16)
    partial_out = jnp.einsum(
        "secf,efd->secd", inner_act, w_down, preferred_element_type=jnp.float32
    ).astype(jnp.bfloat16)
    returned = lax.all_to_all(
        partial_out.reshape(experts, width_slots, model_width),
        "ep",
        split_axis=0,
        concat_axis=0,
        tiled=True,
    )
    returned, arrived, gate_kept, up_kept = (
        returned,
        landed,
        gate_act.reshape(experts, width_slots, -1),
        up_act.reshape(experts, width_slots, -1),
    )
    flat_returned = returned.reshape(experts * capacity, model_width)
    own_pair = jnp.ones_like(kept_float)
    pair_share = kept_float * own_pair
    share_weight = pair_weight * own_pair
    summed = jnp.zeros((own_rows * lax.axis_size("tp"), model_width), jnp.float32)
    for combine_pick_index in range(top_count):
        summed = summed + share_weight[
            :, combine_pick_index : combine_pick_index + 1
        ] * flat_returned[safe_slots[:, combine_pick_index]].astype(jnp.float32)
    moe_own = lax.psum_scatter(
        summed.astype(jnp.bfloat16), "tp", scatter_dimension=0, tiled=True
    ).astype(jnp.float32)
    hidden_own = lax.dynamic_slice_in_dim(hidden_state, first_row, own_rows, 0)
    output = (hidden_own + moe_own).astype(jnp.bfloat16)
    cot_all = lax.all_gather(cotangent, "tp", axis=0, tiled=True)
    cot_float = cot_all.astype(jnp.float32)
    pair_terms = []
    for pick_index in range(top_count):
        picked = flat_returned[safe_slots[:, pick_index]].astype(jnp.float32)
        pair_terms.append(jnp.sum(picked * cot_float, axis=1))
    pair_grad = jnp.stack(pair_terms, axis=1) * pair_share
    route_hits = (routes[:, :, None] == jnp.arange(experts, dtype=jnp.int32)[None, None, :]).astype(
        jnp.float32
    )
    prob_grad = jnp.sum(route_hits * pair_grad[:, :, None], axis=1)
    logit_grad = router_probs * (
        prob_grad - jnp.sum(router_probs * prob_grad, axis=1, keepdims=True)
    )
    router_grad = lax.dot_general(
        normed_moe.astype(jnp.float32),
        logit_grad,
        (((0,), (0,)), ((), ())),
        precision=lax.Precision.HIGHEST,
        preferred_element_type=jnp.float32,
    )
    moe_in_grad = lax.dot_general(
        logit_grad,
        w_router.astype(jnp.float32),
        (((1,), (1,)), ((), ())),
        precision=lax.Precision.HIGHEST,
        preferred_element_type=jnp.float32,
    )
    slot_weight = (
        jnp.zeros((experts * capacity + 1,), jnp.float32)
        .at[slot_ids.reshape(-1)]
        .set(pair_weight.reshape(-1))[: experts * capacity]
    )
    cot_padded = jnp.concatenate([cot_all, zero_row], axis=0)
    grad_out_slots = (
        (cot_padded[slot_token].astype(jnp.float32) * slot_weight[:, None])
        .astype(jnp.bfloat16)
        .reshape(experts, capacity, model_width)
    )
    grad_arrived, inputs_arrived = (
        lax.all_to_all(grad_out_slots, "ep", split_axis=0, concat_axis=0, tiled=True),
        lax.all_to_all(outgoing, "ep", split_axis=0, concat_axis=0, tiled=True),
    )
    grouped_again = inputs_arrived.reshape(ep_size, local_experts, capacity, model_width)
    gate_act = jnp.einsum(
        "secd,edf->secf", grouped_again, w_gate, preferred_element_type=jnp.float32
    )
    up_act = jnp.einsum("secd,edf->secf", grouped_again, w_up, preferred_element_type=jnp.float32)
    grouped_in = inputs_arrived.reshape(ep_size, local_experts, capacity, model_width)
    grouped_grad = grad_arrived.reshape(ep_size, local_experts, capacity, model_width)
    sigmoid_gate = jax.nn.sigmoid(gate_act)
    silu_gate = gate_act * sigmoid_gate
    inner_act = (silu_gate * up_act).astype(jnp.bfloat16)
    grad_w_down = jnp.einsum(
        "secf,secd->efd", inner_act, grouped_grad, preferred_element_type=jnp.float32
    )
    grad_inner = jnp.einsum(
        "secd,efd->secf", grouped_grad, w_down, preferred_element_type=jnp.float32
    )
    grad_up_act = (grad_inner * silu_gate).astype(jnp.bfloat16)
    grad_gate_act = (
        grad_inner * up_act * sigmoid_gate * (1.0 + gate_act * (1.0 - sigmoid_gate))
    ).astype(jnp.bfloat16)
    grad_w_gate = jnp.einsum(
        "secd,secf->edf", grouped_in, grad_gate_act, preferred_element_type=jnp.float32
    )
    grad_w_up = jnp.einsum(
        "secd,secf->edf", grouped_in, grad_up_act, preferred_element_type=jnp.float32
    )
    slot_in_grad = jnp.einsum(
        "secf,edf->secd", grad_gate_act, w_gate, preferred_element_type=jnp.float32
    )
    slot_in_grad = slot_in_grad + jnp.einsum(
        "secf,edf->secd", grad_up_act, w_up, preferred_element_type=jnp.float32
    )
    slot_part = slot_in_grad.astype(jnp.bfloat16).reshape(experts, capacity, model_width)
    flat_back = send_back(slot_part).reshape(experts * capacity, model_width)
    for pick_index in range(top_count):
        moe_in_grad = moe_in_grad + pair_share[:, pick_index : pick_index + 1] * flat_back[
            safe_slots[:, pick_index]
        ].astype(jnp.float32)
    weighted_moe = moe_in_grad * gain_moe
    hidden_part = scale_moe * weighted_moe - hidden_state * scale_moe**3 * jnp.mean(
        hidden_state * weighted_moe, axis=1, keepdims=True
    )
    gain_moe_grad = jnp.sum(hidden_state * scale_moe * moe_in_grad, axis=0)
    hidden_grad = cot_float + lax.psum(hidden_part.astype(jnp.bfloat16), "tp").astype(jnp.float32)
    hidden_low = hidden_grad.astype(jnp.bfloat16)
    grad_w_out = contract_rows(mixed_flat, hidden_low)
    grad_mixed = (
        contract_cols(hidden_low, w_out)
        .astype(jnp.bfloat16)
        .reshape(seq_len, local_heads, head_dim)
    )
    grad_q_rot, grad_k_rot, grad_v_heads = attention_backward(
        q_rot, k_rot, v_heads, grad_mixed, log_total, seg_row, block_rows, score_scale
    )
    grad_q_normed = rotate_back(grad_q_rot, cosine, sine).reshape(seq_len, local_width)
    grad_k_normed = rotate_back(grad_k_rot, cosine, sine).reshape(seq_len, local_width)
    gain_query_grad = jnp.sum(query_unit * grad_q_normed, axis=0).reshape(local_heads, head_dim)
    gain_key_grad = jnp.sum(key_unit * grad_k_normed, axis=0).reshape(local_heads, head_dim)
    weighted_query = grad_q_normed * query_gain
    weighted_key = grad_k_normed * key_gain
    query_inner, key_inner = lax.psum(
        (jnp.sum(queries * weighted_query, axis=1), jnp.sum(key_proj * weighted_key, axis=1)), "tp"
    )
    query_grad = (
        query_scale * weighted_query
        - queries * query_scale**3 * (query_inner / full_width)[:, None]
    ).astype(jnp.bfloat16)
    key_grad = (
        key_scale * weighted_key - key_proj * key_scale**3 * (key_inner / full_width)[:, None]
    ).astype(jnp.bfloat16)
    value_grad = grad_v_heads.reshape(seq_len, local_width).astype(jnp.bfloat16)
    grad_w_query = contract_rows(normed, query_grad)
    grad_w_key = contract_rows(normed, key_grad)
    grad_w_value = contract_rows(normed, value_grad)
    normed_grad = (
        contract_cols(query_grad, w_query)
        + contract_cols(key_grad, w_key)
        + contract_cols(value_grad, w_value)
    )
    weighted_attn = normed_grad * gain_attn
    input_part = scale_attn * weighted_attn - whole_in * scale_attn**3 * jnp.mean(
        whole_in * weighted_attn, axis=1, keepdims=True
    )
    gain_attn_grad = jnp.sum(whole_in * scale_attn * normed_grad, axis=0)

    def spread_rows(vectors):
        pieces = vectors.reshape((ep_size, tp_size, -1) + vectors.shape[1:])
        return jnp.swapaxes(pieces, 0, 1).reshape(vectors.shape)

    input_sum, gain_attn_half, gain_moe_half, router_half = (
        lax.psum_scatter(
            input_part.astype(jnp.bfloat16), "tp", scatter_dimension=0, tiled=True
        ).astype(jnp.float32),
        lax.psum_scatter(
            spread_rows(gain_attn_grad).astype(jnp.bfloat16), "tp", scatter_dimension=0, tiled=True
        ).astype(jnp.float32),
        lax.psum_scatter(
            spread_rows(gain_moe_grad).astype(jnp.bfloat16), "tp", scatter_dimension=0, tiled=True
        ).astype(jnp.float32),
        lax.psum_scatter(
            spread_rows(router_grad).astype(jnp.bfloat16), "tp", scatter_dimension=0, tiled=True
        ).astype(jnp.float32),
    )
    grad_input = lax.dynamic_slice_in_dim(hidden_grad, first_row, own_rows, 0) + input_sum
    reduced = (
        lax.psum_scatter(grad_w_query, "ep", scatter_dimension=0, tiled=True),
        lax.psum_scatter(grad_w_key, "ep", scatter_dimension=0, tiled=True),
        lax.psum_scatter(grad_w_value, "ep", scatter_dimension=0, tiled=True),
        lax.psum_scatter(grad_w_out, "ep", scatter_dimension=1, tiled=True),
        lax.psum_scatter(gain_query_grad, "ep", scatter_dimension=1, tiled=True),
        lax.psum_scatter(gain_key_grad, "ep", scatter_dimension=1, tiled=True),
        lax.psum_scatter(gain_attn_half, "ep", scatter_dimension=0, tiled=True),
        lax.psum_scatter(gain_moe_half, "ep", scatter_dimension=0, tiled=True),
        lax.psum_scatter(router_half, "ep", scatter_dimension=0, tiled=True),
        lax.psum_scatter(route_counts.astype(jnp.float32), "ep", scatter_dimension=0, tiled=True),
    )
    return (
        output,
        grad_input,
        reduced[6],
        reduced[0],
        reduced[1],
        reduced[2],
        reduced[4],
        reduced[5],
        reduced[3],
        reduced[7],
        reduced[8],
        grad_w_gate,
        grad_w_up,
        grad_w_down,
        reduced[9].astype(jnp.int32),
    )


def solution(mesh):
    in_specs = (
        P(("ep", "tp"), None),
        P("ep", None),
        P("ep", None),
        P(),
        P(None, "tp"),
        P(None, "tp"),
        P(None, "tp"),
        P("tp", None),
        P("tp", None),
        P("tp", None),
        P(),
        P(),
        P("ep", None, "tp"),
        P("ep", None, "tp"),
        P("ep", "tp", None),
        P(("ep", "tp"), None),
    )
    out_specs = (
        P(("ep", "tp"), None),
        P(("ep", "tp"), None),
        P(("ep", "tp")),
        P("ep", "tp"),
        P("ep", "tp"),
        P("ep", "tp"),
        P("tp", "ep"),
        P("tp", "ep"),
        P("tp", "ep"),
        P(("ep", "tp")),
        P(("ep", "tp"), None),
        P("ep", None, "tp"),
        P("ep", None, "tp"),
        P("ep", "tp", None),
        P("ep"),
    )
    return jax.shard_map(local, mesh=mesh, in_specs=in_specs, out_specs=out_specs, check_vma=False)
```

profile of v0, /device:TPU:0, one launch (start us, length us, event | category | flops | bytes accessed | tf_op | source)
XLA Modules:
  0.0 2677.1 jit_solution(8424012754544464276)
XLA Ops:
  11.0 12.9 all-gather.3.cloned.1.call-done
  62.3 16.2 all-reduce.16.cloned.1.call-done
  83.1 10.9 gather_fusion
  94.1 108.5 %all_to_all.21 = bf16[64,32,2048]{2,1,0:T(8,128)(2,1)S(1)} all-to-all(bf16[64,32,2048]{2,1,0:T(8,128)(2,1)} %bitcast.265), channel_id=1, replica_groups=mesh['ep'=64,'tp'=2] {'ep'}, dimensions={0} | all-to-all | bytes 16777216 | tf_op jit(solution)/shard_map/all_to_all | solution.py:228
  222.9 9.3 all-to-all-start.1
  233.4 14.3 all-gather.5.cloned.1.call-done
  249.1 11.2 gather_fusion.9
  262.0 86.6 %all-to-all-done.1 = bf16[64,32,2048]{2,1,0:T(8,128)(2,1)} async-done(((bf16[64,32,2048]{2,1,0:T(8,128)(2,1)}), bf16[64,32,2048]{2,1,0:T(8,128)(2,1)}, u32[]{:S(2)}, u32[]{:S(2)}) %all-to-all-start.1) | async-done | bytes 8388640 | tf_op jit(solution)/shard_map/all_to_all | solution.py:237
  372.2 8.2 gather_fusion.5
  418.0 16.8 gather_fusion.18
  451.6 105.9 %all_to_all.22 = bf16[64,32,2048]{2,1,0:T(8,128)(2,1)S(1)} all-to-all(bf16[64,32,2048]{2,1,0:T(8,128)(2,1)} %fusion), channel_id=1, replica_groups=mesh['ep'=64,'tp'=2] {'ep'}, dimensions={0} | all-to-all | bytes 16777216 | tf_op jit(solution)/shard_map/all_to_all | solution.py:304
  565.6 9.9 fusion.45
  575.4 10.8 add_convert_fusion
  586.2 8.6 all-to-all-start.3
  595.9 112.1 %all-to-all-done.3 = bf16[64,32,2048]{2,1,0:T(8,128)(2,1)} async-done(((bf16[64,32,2048]{2,1,0:T(8,128)(2,1)}), bf16[64,32,2048]{2,1,0:T(8,128)(2,1)}, u32[]{:S(2)}, u32[]{:S(2)}) %all-to-all-start.3) | async-done | bytes 8388640 | tf_op jit(solution)/shard_map/all_to_all | solution.py:152
  762.9 8.3 gather_fusion.10
  786.7 18.1 all-reduce.18.cloned.1.call-done
  868.0 9.6 convolution_bitcast_fusion
  877.6 9.9 convolution_bitcast_fusion.1
  896.5 348.9 %all-reduce.9 = (f32[1024]{0:T(1024)S(1)}, f32[8,128]{1,0:T(8,128)S(1)}, f32[8,128]{1,0:T(8,128)S(1)}, f32[1024]{0:T(1024)S(1)}, f32[64]{0:T(128)S(1)}) all-reduce(f32[1024]{0:T(1024)S(1)} %dynamic-slice_convert_fusion.1, f32[8,128]{1,0:T(8,128)S(1)} %bitcast.287, ...), channel_id=5, replica_groups=mesh['ep'=64,'tp'=2] {'ep'}, use_global_device_ids=true, to_apply=%region_41.42.clone | all-reduce | flops 4160 | bytes 33280
  1255.4 316.1 %reduce-scatter.21.cloned.1.call-done = f32[1024,32]{0,1:T(8,128)} async-done(((f32[1024,2048]{0,1:T(8,128)}), f32[1024,32]{0,1:T(8,128)}) %reduce-scatter.21.cloned.1.call-update) | async-done | bytes 131088 | tf_op jit(solution)/shard_map/reduce_scatter | solution.py:415
  1571.5 365.9 %reduce-scatter.19.cloned.1.call-done = f32[32,1024]{1,0:T(8,128)} async-done(((f32[2048,1024]{1,0:T(8,128)}), f32[32,1024]{1,0:T(8,128)}) %reduce-scatter.19.cloned.1.call-update) | async-done | bytes 131088 | tf_op jit(solution)/shard_map/reduce_scatter | solution.py:414
  1937.4 366.1 %reduce-scatter.17.cloned.1.call-done = f32[32,1024]{1,0:T(8,128)} async-done(((f32[2048,1024]{1,0:T(8,128)}), f32[32,1024]{1,0:T(8,128)}) %reduce-scatter.17.cloned.1.call-update) | async-done | bytes 131088 | tf_op jit(solution)/shard_map/reduce_scatter | solution.py:413
  2303.6 365.4 %reduce-scatter.15.cloned.1.call-done = f32[32,1024]{1,0:T(8,128)} async-done(((f32[2048,1024]{1,0:T(8,128)}), f32[32,1024]{1,0:T(8,128)}) %reduce-scatter.15.cloned.1.call-update) | async-done | bytes 131088 | tf_op jit(solution)/shard_map/reduce_scatter | solution.py:412
  (398 shorter events, 307.2 us)
Async XLA Ops:
  7.2 209.0 %copy-start = (bf16[1,512,2048]{2,1,0:T(8,128)(2,1)S(1)}, bf16[1,512,2048]{2,1,0:T(8,128)(2,1)}, u32[]{:S(2)}) copy-start(bf16[1,512,2048]{2,1,0:T(8,128)(2,1)} %param.30) | copy-start | bytes 6291460
  7.2 16.7 all-gather.3.cloned.1.call-start
  7.9 70.6 %all-reduce.16.cloned.1.call-start = ((), (), s32[]{:S(2)}) async-start(), calls=%async_computation.13 | async-start | bytes 4194304 | tf_op jit(solution)/shard_map/psum | solution.py:215
  222.9 125.8 %all-to-all-start.1 = ((bf16[64,32,2048]{2,1,0:T(8,128)(2,1)}), bf16[64,32,2048]{2,1,0:T(8,128)(2,1)}, u32[]{:S(2)}, u32[]{:S(2)}) async-start(bf16[64,32,2048]{2,1,0:T(8,128)(2,1)} %convolution_convert_fusion), calls=%async_computation.1 | async-start | bytes 16777216 | tf_op jit(solution)/shard_map/all_to_all | solution.py:237
  232.2 15.6 all-gather.5.cloned.1.call-start
  233.3 123.2 %copy-start.79 = (s32[1024]{0:T(1024)}, s32[1024]{0:T(1024)S(1)}, u32[]{:S(2)}) copy-start(s32[1024]{0:T(1024)S(1)} %pad_clamp_fusion.1) | copy-start | bytes 12292
  233.3 115.4 %copy-start.86 = (s32[1024]{0:T(1024)}, s32[1024]{0:T(1024)S(1)}, u32[]{:S(2)}) copy-start(s32[1024]{0:T(1024)S(1)} %pad_clamp_fusion) | copy-start | bytes 12292
  233.3 131.0 %copy-start.80 = (s32[1024]{0:T(1024)}, s32[1024]{0:T(1024)S(1)}, u32[]{:S(2)}) copy-start(s32[1024]{0:T(1024)S(1)} %pad_clamp_fusion.2) | copy-start | bytes 12292
  233.3 138.8 %copy-start.81 = (s32[1024]{0:T(1024)}, s32[1024]{0:T(1024)S(1)}, u32[]{:S(2)}) copy-start(s32[1024]{0:T(1024)S(1)} %pad_clamp_fusion.3) | copy-start | bytes 12292
  233.4 147.0 %copy-start.82 = (s32[1024]{0:T(1024)}, s32[1024]{0:T(1024)S(1)}, u32[]{:S(2)}) copy-start(s32[1024]{0:T(1024)S(1)} %pad_clamp_fusion.4) | copy-start | bytes 12292
  233.4 154.8 %copy-start.83 = (s32[1024]{0:T(1024)}, s32[1024]{0:T(1024)S(1)}, u32[]{:S(2)}) copy-start(s32[1024]{0:T(1024)S(1)} %pad_clamp_fusion.5) | copy-start | bytes 12292
  233.4 162.6 %copy-start.84 = (s32[1024]{0:T(1024)}, s32[1024]{0:T(1024)S(1)}, u32[]{:S(2)}) copy-start(s32[1024]{0:T(1024)S(1)} %pad_clamp_fusion.6) | copy-start | bytes 12292
  233.4 170.4 %copy-start.85 = (s32[1024]{0:T(1024)}, s32[1024]{0:T(1024)S(1)}, u32[]{:S(2)}) copy-start(s32[1024]{0:T(1024)S(1)} %pad_clamp_fusion.7) | copy-start | bytes 12292
  586.2 121.8 %all-to-all-start.3 = ((bf16[64,32,2048]{2,1,0:T(8,128)(2,1)}), bf16[64,32,2048]{2,1,0:T(8,128)(2,1)}, u32[]{:S(2)}, u32[]{:S(2)}) async-start(bf16[64,32,2048]{2,1,0:T(8,128)(2,1)} %add_convert_fusion), calls=%async_computation.4 | async-start | bytes 16777216 | tf_op jit(solution)/shard_map/all_to_all | solution.py:152
  594.8 209.9 %all-reduce.18.cloned.1.call-start = ((), (), s32[]{:S(2)}) async-start(), calls=%async_computation.16 | async-start | bytes 2097152 | tf_op jit(solution)/shard_map/psum | solution.py:350
  779.2 58.3 %reduce-scatter.23.cloned.1.call-start = ((), (), s32[]{:S(2)}) async-start(), calls=%async_computation.22 | async-start | bytes 786432 | tf_op jit(solution)/shard_map/reduce_scatter | solution.py:406
  781.9 77.6 %reduce-scatter.11.cloned.1.call-start = ((), (), s32[]{:S(2)}) async-start(), calls=%async_computation.14 | async-start | bytes 1572864 | tf_op jit(solution)/shard_map/reduce_scatter | solution.py:259
  786.6 466.3 %reduce-scatter.13.cloned.1.call-start = ((), (), s32[]{:S(2)}) async-start(), calls=%async_computation.17 | async-start | bytes 1572864 | tf_op jit(solution)/shard_map/reduce_scatter | solution.py:397
  837.4 418.0 %reduce-scatter.25.cloned.1.call-start = ((), (), s32[]{:S(2)}) async-start(), calls=%async_computation.23 | async-start | bytes 532480 | tf_op jit(solution)/shard_map/reduce_scatter | solution.py:420
  839.3 732.2 %reduce-scatter.21.cloned.1.call-start = ((), (), s32[]{:S(2)}) async-start(), calls=%async_computation.21 | async-start | bytes 8519680 | tf_op jit(solution)/shard_map/reduce_scatter | solution.py:415
  845.4 1092.1 %reduce-scatter.19.cloned.1.call-start = ((), (), s32[]{:S(2)}) async-start(), calls=%async_computation.20 | async-start | bytes 8519680 | tf_op jit(solution)/shard_map/reduce_scatter | solution.py:414
  850.1 1453.5 %reduce-scatter.17.cloned.1.call-start = ((), (), s32[]{:S(2)}) async-start(), calls=%async_computation.19 | async-start | bytes 8519680 | tf_op jit(solution)/shard_map/reduce_scatter | solution.py:413
  855.7 1813.2 %reduce-scatter.15.cloned.1.call-start = ((), (), s32[]{:S(2)}) async-start(), calls=%async_computation.18 | async-start | bytes 8519680 | tf_op jit(solution)/shard_map/reduce_scatter | solution.py:412
  1249.9 1419.1 %copy-start.1 = (bf16[1,512,2048]{2,1,0:T(8,128)(2,1)S(1)}, bf16[1,512,2048]{2,1,0:T(8,128)(2,1)}, u32[]{:S(2)}) copy-start(bf16[1,512,2048]{2,1,0:T(8,128)(2,1)} %param.30) | copy-start | bytes 6291460
  (97 other events, 878.5 us)
Sparse Core Ops, SparseCore 0:
  9.7 14.1 all-gather.2
  50.4 28.1 all-reduce.15
  234.8 12.9 all-gather.4
  779.3 25.3 all-reduce.17
  807.0 11.8 reduce-scatter.22
  821.7 12.6 reduce-scatter.10
  837.5 12.4 reduce-scatter.12
  853.0 352.4 reduce-scatter.24
  1208.5 362.9 reduce-scatter.20
  1574.3 363.0 reduce-scatter.18
  1940.4 363.1 reduce-scatter.16
  2306.4 362.5 reduce-scatter.14
where the time goes:
time: 2690 us; the launch traced here: 2680 us
  waiting for transfers between devices  1680 us (62%)
  blocking collectives  571 us (21%)
  local copies, waits for them, and re-layouts  214 us (8%)
  matrix products  128 us (5%)
  other arithmetic  51.1 us (2%)
    reduce_scatter x1, waiting for transfers between devices, local(): lax.psum_scatter(grad_w_key, 'ep', scatter_dimension=0, tiled=True)  366 us
    reduce_scatter x1, waiting for transfers between devices, local(): lax.psum_scatter(grad_w_value, 'ep', scatter_dimension=0, tiled=True)  366 us
    reduce_scatter x1, waiting for transfers between devices, local(): lax.psum_scatter(grad_w_query, 'ep', scatter_dimension=0, tiled=True)  365 us
    unnamed x2, blocking collectives  351 us
    reduce_scatter x1, waiting for transfers between devices, local(): lax.psum_scatter(grad_w_out, 'ep', scatter_dimension=1, tiled=True)  316 us
    all_to_all x1, waiting for transfers between devices, send_back(): lax.all_to_all(slot_grads, 'ep', split_axis=0, concat_axis=0, tiled=True)  112 us
    all_to_all x1, blocking collectives, local(): lax.all_to_all(outgoing, 'ep', split_axis=0, concat_axis=0, tiled=True)  108 us
    all_to_all x1, blocking collectives, local(): lax.all_to_all(grad_out_slots, 'ep', split_axis=0, concat_axis=0, tiled=T...  106 us
  transfers between devices with their start and end apart: 14, of which 10 were waited for; matrix products, arithmetic and copies ran while one was open for 5% of the time, Pallas kernels for 0%

commit v1 on v0

v1 whole, which is shorter than its diff:
```python
import jax
import jax.numpy as jnp
from jax import lax
from jax.sharding import Mesh, PartitionSpec as P

norm_eps = 1e-05
rope_base = 10000.0
mask_fill = -1e30
bf16 = jnp.bfloat16
f32 = jnp.float32
rows_of_chips = ("z", "x", "y")


def swap(value):
    return lax.ppermute(value, "tp", [(0, 1), (1, 0)])


def dot(left, right):
    return lax.dot_general(left, right, (((1,), (0,)), ((), ())), preferred_element_type=f32)


def dot_rows(left, right):
    return lax.dot_general(left, right, (((0,), (0,)), ((), ())), preferred_element_type=f32)


def dot_cols(left, right):
    return lax.dot_general(left, right, (((1,), (1,)), ((), ())), preferred_element_type=f32)


def all_to_all(value, axes):
    return lax.all_to_all(value, axes, split_axis=0, concat_axis=0, tiled=True)


def rms_scale(values):
    return lax.rsqrt(jnp.mean(values * values, axis=-1, keepdims=True) + norm_eps)


def halves(value):
    high = value.astype(bf16)
    return high, (value - high.astype(f32)).astype(bf16)


def rope_angles(positions, head_dim):
    half_dim = head_dim // 2
    exponent = jnp.arange(half_dim, dtype=f32) * (2.0 / head_dim)
    inverse = jnp.power(f32(rope_base), -exponent)
    angles = positions.astype(f32)[:, None] * inverse[None, :]
    return jnp.cos(angles), jnp.sin(angles)


def rotate(values, cosine, sine):
    half_dim = values.shape[-1] // 2
    first_half = values[..., :half_dim]
    second_half = values[..., half_dim:]
    cos_b = cosine[:, None, :]
    sin_b = sine[:, None, :]
    return jnp.concatenate(
        [first_half * cos_b - second_half * sin_b, second_half * cos_b + first_half * sin_b],
        axis=-1,
    )


def local(
    residual_in,
    routes,
    segment_ids,
    gain_attn,
    w_query,
    w_key,
    w_value,
    gain_query,
    gain_key,
    w_out,
    gain_moe,
    w_router,
    w_gate,
    w_up,
    w_down,
    cotangent,
):
    core = lax.axis_index("tp")
    planes = lax.axis_size("z")
    chips = lax.axis_size(rows_of_chips)
    chip = lax.axis_index(rows_of_chips)
    own_rows, width = residual_in.shape
    seq_len, top_count = routes.shape
    local_width = w_query.shape[1]
    local_heads, head_dim = gain_query.shape
    full_width = 2 * local_width
    experts = chips
    capacity = seq_len * top_count // experts
    own_slots = capacity // 2
    score_scale = head_dim ** (-0.5)
    quarter = local_width // planes
    out_rows = width // chips

    def own_first(value):
        return jnp.where(
            core == 0, value, jnp.concatenate([value[own_rows:], value[:own_rows]], axis=0)
        )

    def other_order(value):
        return jnp.concatenate([value[own_rows:], value[:own_rows]], axis=0)

    place = own_first(jnp.arange(seq_len, dtype=jnp.int32))
    seg = own_first(segment_ids[0])
    route = own_first(routes)
    same_doc = seg[:, None] == seg[None, :]
    position = place - jnp.min(jnp.where(same_doc, place[None, :], seq_len), axis=1)
    cosine, sine = rope_angles(position, head_dim)
    allowed = same_doc & (place[None, :] <= place[:, None])

    hits = jnp.any(
        route[:, :, None] == jnp.arange(experts, dtype=jnp.int32)[None, None, :], axis=1
    )
    before = (place[None, :] < place[:, None]).astype(bf16)
    rank = dot(before, hits.astype(bf16)).astype(jnp.int32)
    rank = jnp.where(hits, rank, -1)
    counts = jnp.sum(hits.astype(f32), axis=0)
    slot_number = core * own_slots + jnp.arange(own_slots, dtype=jnp.int32)
    pick = (rank.T[:, None, :] == slot_number[None, :, None]).astype(bf16)
    pick = pick.reshape(experts * own_slots, seq_len)

    cot = jnp.concatenate([cotangent, swap(cotangent)], axis=0)
    cot_slots = dot(pick, cot).astype(bf16).reshape(experts, own_slots, width)
    cot_arrived = all_to_all(cot_slots, rows_of_chips).reshape(experts * own_slots, width)

    whole_in = jnp.concatenate([residual_in, swap(residual_in)], axis=0).astype(f32)
    scale_attn = rms_scale(whole_in)
    normed = (whole_in * scale_attn * gain_attn).astype(bf16)
    normed_own = normed[:own_rows]
    normed_planes = lax.all_gather(normed_own, "z", axis=0, tiled=False)
    normed_planes = jnp.concatenate([normed_planes, swap(normed_planes)], axis=1).reshape(
        planes * seq_len, width
    )
    queries = dot(normed, w_query)
    key_proj = dot(normed, w_key)
    values = dot(normed, w_value).astype(bf16)
    squares = jnp.stack([jnp.sum(queries * queries, axis=1), jnp.sum(key_proj * key_proj, axis=1)])
    squares = squares + other_order(swap(squares).T).T
    query_scale = lax.rsqrt(squares[0] / full_width + norm_eps)[:, None]
    key_scale = lax.rsqrt(squares[1] / full_width + norm_eps)[:, None]
    query_gain = gain_query.reshape(-1)
    key_gain = gain_key.reshape(-1)
    heads = (seq_len, local_heads, head_dim)
    q_rot = rotate((queries * query_scale * query_gain).reshape(heads), cosine, sine).astype(bf16)
    k_rot = rotate((key_proj * key_scale * key_gain).reshape(heads), cosine, sine).astype(bf16)
    v_heads = values.reshape(heads)
    scores = jnp.einsum("qhd,khd->hqk", q_rot, k_rot, preferred_element_type=f32) * score_scale
    scores = jnp.where(allowed[None], scores, mask_fill)
    grown = jnp.exp(scores - jnp.max(scores, axis=-1, keepdims=True))
    probs = grown / jnp.sum(grown, axis=-1, keepdims=True)
    probs_low = probs.astype(bf16)
    mixed = (
        jnp.einsum("hqk,khd->qhd", probs_low, v_heads, preferred_element_type=f32)
        .reshape(seq_len, local_width)
        .astype(bf16)
    )
    mixed_planes = all_to_all(
        jnp.stack([mixed[:, k * quarter : (k + 1) * quarter] for k in range(planes)]), "z"
    ).reshape(planes * seq_len, quarter)
    branch = dot(mixed, w_out)
    branch = branch + other_order(swap(branch))
    hidden = whole_in + branch
    scale_moe = rms_scale(hidden)
    normed_moe = (hidden * scale_moe * gain_moe).astype(bf16)

    moe_slots = dot(pick, normed_moe).astype(bf16).reshape(experts, own_slots, width)
    arrived = all_to_all(moe_slots, rows_of_chips).reshape(experts * own_slots, width)
    router_probs = jax.nn.softmax(dot(normed_moe, w_router), axis=-1)

    gate_parts = (w_gate[0], swap(w_gate[0]))
    up_parts = (w_up[0], swap(w_up[0]))
    down_parts = (w_down[0], swap(w_down[0]))
    slot_probs = jax.nn.softmax(dot(arrived, w_router), axis=-1)
    own_expert = jnp.arange(experts, dtype=jnp.int32) == chip
    slot_weight = jnp.sum(jnp.where(own_expert[None, :], slot_probs, 0.0), axis=1, keepdims=True)
    slot_grad = (slot_weight * cot_arrived.astype(f32)).astype(bf16)
    saved = []
    slot_out = None
    for w_g, w_u, w_d in zip(gate_parts, up_parts, down_parts):
        gate_act = dot(arrived, w_g)
        up_act = dot(arrived, w_u)
        sigmoid_gate = jax.nn.sigmoid(gate_act)
        silu_gate = gate_act * sigmoid_gate
        inner_act = (silu_gate * up_act).astype(bf16)
        part_out = dot(inner_act, w_d)
        slot_out = part_out if slot_out is None else slot_out + part_out
        saved.append((gate_act, up_act, sigmoid_gate, silu_gate, inner_act))
    returned = all_to_all(
        slot_out.astype(bf16).reshape(experts, own_slots, width), rows_of_chips
    ).reshape(experts * own_slots, width)
    part_grads = []
    slot_in_grad = None
    for (gate_act, up_act, sigmoid_gate, silu_gate, inner_act), w_g, w_u, w_d in zip(
        saved, gate_parts, up_parts, down_parts
    ):
        inner_grad = dot_cols(slot_grad, w_d)
        up_grad = (inner_grad * silu_gate).astype(bf16)
        gate_grad = (
            inner_grad * up_act * sigmoid_gate * (1.0 + gate_act * (1.0 - sigmoid_gate))
        ).astype(bf16)
        part_in = dot_cols(gate_grad, w_g) + dot_cols(up_grad, w_u)
        slot_in_grad = part_in if slot_in_grad is None else slot_in_grad + part_in
        part_grads.append((inner_act, gate_grad, up_grad))
    grads_back = all_to_all(
        slot_in_grad.astype(bf16).reshape(experts, own_slots, width), rows_of_chips
    ).reshape(experts * own_slots, width)
    (inner_own, gate_own, up_own), (inner_other, gate_other, up_other) = part_grads
    grad_w_gate = dot_rows(arrived, gate_own) + swap(
        dot_rows(arrived, gate_other).astype(bf16)
    ).astype(f32)
    grad_w_up = dot_rows(arrived, up_own) + swap(dot_rows(arrived, up_other).astype(bf16)).astype(
        f32
    )
    grad_w_down = dot_rows(inner_own, slot_grad) + swap(
        dot_rows(inner_other, slot_grad).astype(bf16)
    ).astype(f32)

    pick_pairs = pick.reshape(experts, own_slots, seq_len)
    weighted = pick_pairs.astype(f32) * router_probs.T[:, None, :]
    weight_high, weight_low = halves(weighted.reshape(experts * own_slots, seq_len))
    moe_part = dot_rows(weight_high, returned) + dot_rows(weight_low, returned)
    moe_own = moe_part[:own_rows] + swap(moe_part[own_rows:].astype(bf16)).astype(f32)
    output = (hidden[:own_rows] + moe_own).astype(bf16)
    pair_products = dot_cols(returned, cot).reshape(experts, own_slots, seq_len)
    prob_part = jnp.sum(pair_products * pick_pairs.astype(f32), axis=1).T
    prob_grad = prob_part + other_order(swap(prob_part))
    logit_grad = router_probs * (
        prob_grad - jnp.sum(router_probs * prob_grad, axis=1, keepdims=True)
    )
    logit_high, logit_low = halves(logit_grad)
    router_grad = dot_rows(normed_moe, logit_high) + dot_rows(normed_moe, logit_low)
    moe_in_part = dot_rows(pick, grads_back)
    moe_in_grad = (
        moe_in_part[:own_rows]
        + swap(moe_in_part[own_rows:])
        + dot_cols(logit_high[:own_rows], w_router)
        + dot_cols(logit_low[:own_rows], w_router)
    )
    cot_own = cotangent.astype(f32)
    hidden_own = hidden[:own_rows]
    scale_own = scale_moe[:own_rows]
    weighted_moe = moe_in_grad * gain_moe
    hidden_grad = (
        cot_own
        + scale_own * weighted_moe
        - hidden_own * scale_own**3 * jnp.mean(hidden_own * weighted_moe, axis=1, keepdims=True)
    )
    gain_moe_grad = jnp.sum(hidden_own * scale_own * moe_in_grad, axis=0)
    hidden_low_own = hidden_grad.astype(bf16)
    hidden_low = jnp.concatenate([hidden_low_own, swap(hidden_low_own)], axis=0)

    low_planes = lax.all_gather(hidden_low_own, "z", axis=0, tiled=False)
    low_planes = jnp.concatenate([low_planes, swap(low_planes)], axis=1).reshape(
        planes * seq_len, width
    )

    def for_cores(vector):
        pieces = vector.reshape(chips, 2, -1)
        mine = jnp.where(core == 0, pieces[:, 0], pieces[:, 1])
        others = jnp.where(core == 0, pieces[:, 1], pieces[:, 0])
        return mine + swap(others)

    lanes = 128

    def lane_blocks(matrix):
        pieces = matrix.reshape(chips, -1, matrix.shape[1])
        return [
            pieces[:, :, k * lanes : (k + 1) * lanes] for k in range(matrix.shape[1] // lanes)
        ]

    def small_rows(values):
        high, low = halves(jnp.pad(values, ((0, 0), (0, lanes - values.shape[1]))))
        return jnp.pad(jnp.stack([high, low], axis=1), ((0, 0), (0, 14), (0, 0)))

    out_grad = dot_rows(low_planes, mixed_planes).astype(bf16)
    router_pieces = router_grad.reshape(chips, 2, out_rows // 2, experts)
    router_mine = jnp.where(core == 0, router_pieces[:, 0], router_pieces[:, 1])
    router_mine = router_mine.reshape(chips, -1, lanes).astype(bf16)
    router_len = router_mine.shape[1]
    first_small = small_rows(
        jnp.concatenate([for_cores(gain_moe_grad), counts[:, None]], axis=1)
    )
    first_parcel = jnp.concatenate(lane_blocks(out_grad) + [router_mine, first_small], axis=1)
    first_sums = all_to_all(first_parcel, rows_of_chips).astype(f32)
    first_sums = jnp.sum(
        first_sums.reshape((planes, chips // planes) + first_sums.shape[1:]), axis=1
    )

    grad_mixed = dot_cols(hidden_low, w_out).astype(bf16).reshape(heads)
    grad_probs = jnp.einsum("qhd,khd->hqk", grad_mixed, v_heads, preferred_element_type=f32)
    grad_scores = (
        probs * (grad_probs - jnp.sum(probs * grad_probs, axis=-1, keepdims=True))
    ).astype(bf16)
    grad_q_rot = (
        jnp.einsum("hqk,khd->qhd", grad_scores, k_rot, preferred_element_type=f32) * score_scale
    )
    grad_k_rot = (
        jnp.einsum("hqk,qhd->khd", grad_scores, q_rot, preferred_element_type=f32) * score_scale
    )
    value_grad = (
        jnp.einsum("hqk,qhd->khd", probs_low, grad_mixed, preferred_element_type=f32)
        .reshape(seq_len, local_width)
        .astype(bf16)
    )
    grad_q_normed = rotate(grad_q_rot, cosine, -sine).reshape(seq_len, local_width)
    grad_k_normed = rotate(grad_k_rot, cosine, -sine).reshape(seq_len, local_width)
    gain_query_grad = jnp.sum(queries * query_scale * grad_q_normed, axis=0)
    gain_key_grad = jnp.sum(key_proj * key_scale * grad_k_normed, axis=0)
    weighted_query = grad_q_normed * query_gain
    weighted_key = grad_k_normed * key_gain
    inner = jnp.stack(
        [jnp.sum(queries * weighted_query, axis=1), jnp.sum(key_proj * weighted_key, axis=1)]
    )
    inner = (inner + other_order(swap(inner).T).T) / full_width
    query_grad = (
        query_scale * weighted_query - queries * query_scale**3 * inner[0][:, None]
    ).astype(bf16)
    key_grad = (
        key_scale * weighted_key - key_proj * key_scale**3 * inner[1][:, None]
    ).astype(bf16)

    to_planes = jnp.stack(
        [
            jnp.concatenate(
                [g[:, k * quarter : (k + 1) * quarter] for g in (query_grad, key_grad, value_grad)],
                axis=1,
            )
            for k in range(planes)
        ]
    )
    grads_planes = all_to_all(to_planes, "z").reshape(planes * seq_len, 3 * quarter)
    in_grads = dot_rows(normed_planes, grads_planes).astype(bf16)
    normed_grad = (
        dot_cols(query_grad, w_query) + dot_cols(key_grad, w_key) + dot_cols(value_grad, w_value)
    )
    normed_grad = normed_grad[:own_rows] + swap(normed_grad[own_rows:])
    in_own = whole_in[:own_rows]
    in_scale = scale_attn[:own_rows]
    weighted_attn = normed_grad * gain_attn
    grad_input = (
        hidden_grad
        + in_scale * weighted_attn
        - in_own * in_scale**3 * jnp.mean(in_own * weighted_attn, axis=1, keepdims=True)
    )
    gain_attn_grad = jnp.sum(in_own * in_scale * normed_grad, axis=0)

    def by_lane(vector):
        pieces = vector.reshape(local_heads, chips, head_dim // chips)
        return jnp.swapaxes(pieces, 0, 1).reshape(chips, -1)

    last_small = small_rows(
        jnp.concatenate(
            [for_cores(gain_attn_grad), by_lane(gain_query_grad), by_lane(gain_key_grad)], axis=1
        )
    )
    last_parcel = jnp.concatenate(lane_blocks(in_grads) + [last_small], axis=1)
    last_sums = all_to_all(last_parcel, rows_of_chips).astype(f32)
    last_sums = jnp.sum(last_sums.reshape((planes, chips // planes) + last_sums.shape[1:]), axis=1)

    def matrix_of(blocks):
        pieces = blocks.reshape(planes, -1, out_rows, lanes)
        return jnp.transpose(pieces, (2, 0, 1, 3)).reshape(out_rows, -1)

    block_len = quarter // lanes * out_rows
    grad_w_query, grad_w_key, grad_w_value = (
        matrix_of(last_sums[:, k * block_len : (k + 1) * block_len]) for k in range(3)
    )
    grad_w_out = matrix_of(first_sums[:, :block_len]).T
    grad_w_router = jnp.sum(first_sums[:, block_len : block_len + router_len], axis=0).reshape(
        out_rows // 2, experts
    )
    first_tail = jnp.sum(first_sums[:, block_len + router_len :], axis=0)
    first_tail = first_tail[0] + first_tail[1]
    last_tail = jnp.sum(last_sums[:, 3 * block_len :], axis=0)
    last_tail = last_tail[0] + last_tail[1]
    own_gain = out_rows // 2
    own_lanes = local_heads * head_dim // chips
    lane_shape = (local_heads, head_dim // chips)
    return (
        output,
        grad_input,
        last_tail[:own_gain],
        grad_w_query,
        grad_w_key,
        grad_w_value,
        last_tail[own_gain : own_gain + own_lanes].reshape(lane_shape),
        last_tail[own_gain + own_lanes : own_gain + 2 * own_lanes].reshape(lane_shape),
        grad_w_out,
        first_tail[:own_gain],
        grad_w_router,
        grad_w_gate[None],
        grad_w_up[None],
        grad_w_down[None],
        first_tail[own_gain : own_gain + 1].astype(jnp.int32),
    )


def solution(mesh):
    side = round(mesh.shape["ep"] ** (1 / 3))
    cube = Mesh(mesh.devices.reshape(side, side, side, 2), rows_of_chips + ("tp",))
    ep = rows_of_chips
    both = rows_of_chips + ("tp",)
    in_specs = (
        P(both, None),
        P(ep, None),
        P(ep, None),
        P(),
        P(None, "tp"),
        P(None, "tp"),
        P(None, "tp"),
        P("tp", None),
        P("tp", None),
        P("tp", None),
        P(),
        P(),
        P(ep, None, "tp"),
        P(ep, None, "tp"),
        P(ep, "tp", None),
        P(both, None),
    )
    out_specs = (
        P(both, None),
        P(both, None),
        P(both),
        P(ep, "tp"),
        P(ep, "tp"),
        P(ep, "tp"),
        P("tp", ep),
        P("tp", ep),
        P("tp", ep),
        P(both),
        P(both, None),
        P(ep, None, "tp"),
        P(ep, None, "tp"),
        P(ep, "tp", None),
        P(ep),
    )
    return jax.shard_map(local, mesh=cube, in_specs=in_specs, out_specs=out_specs, check_vma=False)
```

time: 2690 us -> 577 us (0.21)
  waiting for transfers between devices: 1680 us -> 202 us
  blocking collectives: 571 us -> 0 us
  local copies, waits for them, and re-layouts: 214 us -> 57.1 us
  matrix products: 128 us -> 179 us
  starting transfers between devices: 19 us -> 68 us
    reduce_scatter x8 -> x0, waiting for transfers between devices: 1410 us -> none  [the longest x1 366 us: local(): lax.psum_scatter(grad_w_key, 'ep', scatter_dimension=0, tiled=True)]
    unnamed x2 -> x0, blocking collectives: 351 us -> none
    all_to_all x2 -> x0, blocking collectives: 214 us -> none  [the longest x1 108 us: local(): lax.all_to_all(outgoing, 'ep', split_axis=0, concat_axis=0, tiled=True)]
    gather x23 -> x0, local copies, waits for them, and re-layouts: 166 us -> none  [the longest x8 63.2 us: local(): flat_back[safe_slots[:, pick_index]].astype(jnp.float32)]
    dot_general x30 -> x46, matrix products: 128 us -> 176 us  [the longest x13 61.6 us: dot_rows(): lax.dot_general(left, right, (((0,), (0,)), ((), ())), preferred_element_...]
    all_to_all x2 -> x8, waiting for transfers between devices: 199 us -> 152 us  [all_to_all(): return lax.all_to_all(value, axes, split_axis=0, concat_axis=0, tiled=True)]
    all_to_all x2 -> x8, starting transfers between devices: 17.9 us -> 62.8 us  [all_to_all(): return lax.all_to_all(value, axes, split_axis=0, concat_axis=0, tiled=True)]
    psum x2 -> x0, waiting for transfers between devices: 34.3 us -> none  [the longest x1 18.1 us: local(): lax.psum(hidden_part.astype(jnp.bfloat16), 'tp').astype(jnp.float32)]
  transfers between devices with their start and end apart: 14 -> 30, of which waited for: 10 -> 11; matrix products, arithmetic and copies ran while one was open for 5% -> 40% of each run, Pallas kernels for 0% -> 0%
where the time goes in v1:
time: 577 us; the launch traced here: 567 us
  waiting for transfers between devices  202 us (35%)
  matrix products  179 us (31%)
  starting transfers between devices  68 us (12%)
  local copies, waits for them, and re-layouts  57.1 us (10%)
  other arithmetic  44.1 us (8%)
  between operations  17.7 us (3%)
    all_to_all x8, waiting for transfers between devices, all_to_all(): return lax.all_to_all(value, axes, split_axis=0, concat_axis=0, tiled=True)  152 us
    all_to_all x8, starting transfers between devices, all_to_all(): return lax.all_to_all(value, axes, split_axis=0, concat_axis=0, tiled=True)  62.8 us
    dot_general x13, matrix products, dot_rows(): lax.dot_general(left, right, (((0,), (0,)), ((), ())), preferred_element_...  61.6 us
    dot_general x13, matrix products, dot_cols(): lax.dot_general(left, right, (((1,), (1,)), ((), ())), preferred_element_...  55.4 us
    dot_general x15, matrix products, dot(): lax.dot_general(left, right, (((1,), (0,)), ((), ())), preferred_element_...  53.5 us
    all_gather x1, waiting for transfers between devices, local(): normed_planes = lax.all_gather(normed_own, 'z', axis=0, tiled=False)  42.7 us
    unnamed x201, local copies, waits for them, and re-layouts  23.3 us
  transfers between devices with their start and end apart: 30, of which 11 were waited for; matrix products, arithmetic and copies ran while one was open for 40% of the time, Pallas kernels for 0%

profile of v1, /device:TPU:0, one launch (start us, length us, event | category | flops | bytes accessed | tf_op | source)
XLA Modules:
  0.0 567.0 jit_solution(12383538196646221065)
XLA Ops:
  45.6 11.9 %all-to-all-start = ((bf16[64,16,2048]{2,1,0:T(8,128)(2,1)}), bf16[64,16,2048]{2,1,0:T(8,128)(2,1)}, u32[]{:S(2)}, u32[]{:S(2)}) async-start(bf16[64,16,2048]{2,1,0:T(8,128)(2,1)} %bitcast.293), calls=%async_computation | async-start | bytes 8388608 | tf_op jit(solution)/shard_map/all_to_all | solution.py:31
  63.8 48.4 %all-to-all-done = bf16[64,16,2048]{2,1,0:T(8,128)(2,1)} async-done(((bf16[64,16,2048]{2,1,0:T(8,128)(2,1)}), bf16[64,16,2048]{2,1,0:T(8,128)(2,1)}, u32[]{:S(2)}, u32[]{:S(2)}) %all-to-all-start) | async-done | bytes 4194336 | tf_op jit(solution)/shard_map/all_to_all | solution.py:31
  112.2 6.6 %all-to-all-start.2 = ((bf16[64,16,2048]{2,1,0:T(8,128)(2,1)}), bf16[64,16,2048]{2,1,0:T(8,128)(2,1)}, u32[]{:S(2)}, u32[]{:S(2)}) async-start(bf16[64,16,2048]{2,1,0:T(8,128)(2,1)} %bitcast.292), calls=%async_computation.2 | async-start | bytes 8388608 | tf_op jit(solution)/shard_map/all_to_all | solution.py:31
  123.4 6.5 %fusion.107 = f32[1024,512]{1,0:T(8,128)} fusion(bf16[1024,2048]{1,0:T(8,128)(2,1)} %bitcast.18, bf16[1,2048,512]{2,1,0:T(8,128)(2,1)} %param.29), kind=kOutput, calls=%fused_computation.255 | convolution fusion | flops 2147483648 | bytes 8388608 | tf_op jit(solution)/shard_map/dot_general | solution.py:19
  130.0 42.1 %all-to-all-done.2 = bf16[64,16,2048]{2,1,0:T(8,128)(2,1)} async-done(((bf16[64,16,2048]{2,1,0:T(8,128)(2,1)}), bf16[64,16,2048]{2,1,0:T(8,128)(2,1)}, u32[]{:S(2)}, u32[]{:S(2)}) %all-to-all-start.2) | async-done | bytes 4194336 | tf_op jit(solution)/shard_map/all_to_all | solution.py:31
  195.1 5.9 %fusion.142 = f32[1024,512]{1,0:T(8,128)S(1)} fusion(bf16[1024,2048]{1,0:T(8,128)(2,1)S(1)} %fusion.1, bf16[512,2048]{1,0:T(8,128)(2,1)} %collective-permute-done.5), kind=kOutput, calls=%fused_computation.290 | convolution fusion | flops 2147483648 | bytes 8388608 | tf_op jit(solution)/shard_map/dot_general | solution.py:27
  201.0 7.6 %multiply_convert_fusion.3 = (bf16[1024,512]{1,0:T(8,128)(2,1)}, bf16[1024,512]{1,0:T(8,128)(2,1)}, bf16[1024,512]{1,0:T(8,128)(2,1)S(1)}) fusion(f32[1024,512]{1,0:T(8,128)S(1)} %fusion.142, f32[1024,512]{1,0:T(8,128)S(1)} %fusion.141, bf16[1024,2048]{1,0:T(8,128)(2,1)} %bitcast.18, bf16[2048,512]{1,0:T(8,128)(2,1)} %collective-permute-done.3), kind=kOutput, calls=%fused_computation.41 | convolution fusion | flops 2155347968 | bytes 13631488 | tf_op jit(solution)/shard_map/dot_general | solution.py:19
  208.6 6.4 %add_convert_fusion.1 = bf16[1024,2048]{1,0:T(8,128)(2,1)} fusion(f32[1024,2048]{1,0:T(8,128)S(1)} %fusion.103, bf16[1024,512]{1,0:T(8,128)(2,1)S(1)} %get-tuple-element.123, bf16[512,2048]{1,0:T(8,128)(2,1)} %collective-permute-done.5), kind=kOutput, calls=%fused_computation.5 | convolution fusion | flops 2151677952 | bytes 15728640 | tf_op jit(solution)/shard_map/dot_general | solution.py:19
  215.0 7.1 %all-to-all-start.1 = ((bf16[64,16,2048]{2,1,0:T(8,128)(2,1)}), bf16[64,16,2048]{2,1,0:T(8,128)(2,1)}, u32[]{:S(2)}, u32[]{:S(2)}) async-start(bf16[64,16,2048]{2,1,0:T(8,128)(2,1)} %bitcast.297), calls=%async_computation.1 | async-start | bytes 8388608 | tf_op jit(solution)/shard_map/all_to_all | solution.py:31
  235.6 7.4 %fusion.143 = f32[1024,2048]{1,0:T(8,128)} fusion(bf16[1024,512]{1,0:T(8,128)(2,1)S(1)} %copy-done.84, bf16[2048,512]{1,0:T(8,128)(2,1)} %collective-permute-done.4), kind=kOutput, calls=%fused_computation.291 | convolution fusion | flops 2147483648 | bytes 11534336 | tf_op jit(solution)/shard_map/dot_general | solution.py:27
  243.0 11.8 %add_convert_fusion = bf16[1024,2048]{1,0:T(8,128)(2,1)} fusion(f32[1024,2048]{1,0:T(8,128)} %fusion.143, f32[1024,2048]{1,0:T(8,128)} %fusion.109, f32[1024,2048]{1,0:T(8,128)S(1)} %fusion.105, bf16[1024,512]{1,0:T(8,128)(2,1)} %get-tuple-element.121, bf16[2048,512]{1,0:T(8,128)(2,1)} %collective-permute-done.3), kind=kOutput, calls=%fused_computation.3 | convolution fusion | flops 2155872256 | bytes 32505856 | tf_op jit(solution)/shard_map/dot_general | solution.py:27
  254.8 18.6 %all-to-all-done.1 = bf16[64,16,2048]{2,1,0:T(8,128)(2,1)} async-done(((bf16[64,16,2048]{2,1,0:T(8,128)(2,1)}), bf16[64,16,2048]{2,1,0:T(8,128)(2,1)}, u32[]{:S(2)}, u32[]{:S(2)}) %all-to-all-start.1) | async-done | bytes 4194336 | tf_op jit(solution)/shard_map/all_to_all | solution.py:31
  273.4 7.4 %all-to-all-start.3 = ((bf16[64,16,2048]{2,1,0:T(8,128)(2,1)}), bf16[64,16,2048]{2,1,0:T(8,128)(2,1)}, u32[]{:S(2)}, u32[]{:S(2)}) async-start(bf16[64,16,2048]{2,1,0:T(8,128)(2,1)} %bitcast.294), calls=%async_computation.3 | async-start | bytes 8388608 | tf_op jit(solution)/shard_map/all_to_all | solution.py:31
  287.1 42.7 %all-gather.5.cloned.1.call-done = bf16[512,2048]{1,0:T(8,128)(2,1)} async-done(((bf16[128,2048]{1,0:T(8,128)(2,1)}), bf16[512,2048]{1,0:T(8,128)(2,1)}) %all-gather.5.cloned.1.call-update) | async-done | bytes 2097168 | tf_op jit(solution)/shard_map/all_gather | solution.py:132
  333.8 6.0 %convolution_convert_fusion.2 = bf16[512,2048]{1,0:T(8,128)(2,1)} fusion(bf16[1024,512]{1,0:T(8,128)(2,1)S(1)} %copy-done.87, bf16[1024,2048]{1,0:T(8,128)(2,1)} %copy-done.3), kind=kOutput, calls=%fused_computation.21 | convolution fusion | flops 2148532224 | bytes 7340032 | tf_op jit(solution)/shard_map/dot_general | solution.py:23
  346.4 6.0 %convolution_convert_fusion.4 = bf16[2048,512]{1,0:T(8,128)(2,1)} fusion(bf16[1024,2048]{1,0:T(8,128)(2,1)} %bitcast.18, bf16[1024,512]{1,0:T(8,128)(2,1)S(1)} %copy-done.35), kind=kOutput, calls=%fused_computation.23 | convolution fusion | flops 2148532224 | bytes 7340032 | tf_op jit(solution)/shard_map/dot_general | solution.py:23
  373.7 6.9 %add_bitcast_fusion = f32[1,512,2048]{2,1,0:T(8,128)} fusion(bf16[512,2048]{1,0:T(8,128)(2,1)S(1)} %collective-permute-done.19, bf16[1024,512]{1,0:T(8,128)(2,1)} %copy-done.36, bf16[1024,2048]{1,0:T(8,128)(2,1)} %copy-done.3), kind=kOutput, calls=%fused_computation.16 | convolution fusion | flops 2149580800 | bytes 11534336 | tf_op jit(solution)/shard_map/dot_general | solution.py:23
  426.9 7.6 %add_bitcast_fusion.1 = f32[1,2048,512]{2,1,0:T(8,128)} fusion(bf16[2048,512]{1,0:T(8,128)(2,1)} %collective-permute-done.18, bf16[1024,2048]{1,0:T(8,128)(2,1)} %bitcast.18, bf16[1024,512]{1,0:T(8,128)(2,1)} %get-tuple-element.124), kind=kOutput, calls=%fused_computation.17 | convolution fusion | flops 2149580800 | bytes 11534336 | tf_op jit(solution)/shard_map/dot_general | solution.py:23
  449.4 6.1 %bitcast_convert_fusion = bf16[2048,768]{1,0:T(8,128)(2,1)S(1)} fusion(bf16[4,256,768]{2,1,0:T(8,128)(2,1)} %all-to-all-done.4, bf16[4,128,2048]{1,2,0:T(8,128)(2,1)} %collective-permute-done.13, bf16[4,128,2048]{1,2,0:T(8,128)(2,1)} %copy.306), kind=kOutput, calls=%fused_computation.7 | convolution fusion | flops 3231186944 | bytes 8912896 | tf_op jit(solution)/shard_map/dot_general | solution.py:23
  465.8 13.0 %all-to-all-start.5 = ((bf16[64,208,128]{2,1,0:T(8,128)(2,1)}), bf16[64,208,128]{2,1,0:T(8,128)(2,1)}, u32[]{:S(2)}, u32[]{:S(2)}) async-start(bf16[64,208,128]{2,1,0:T(8,128)(2,1)} %pad_dynamic-update-slice_fusion), calls=%async_computation.5 | async-start | bytes 6815744 | tf_op jit(solution)/shard_map/all_to_all | solution.py:31
  478.8 7.6 %add_bitcast_fusion.2 = f32[1,2048,512]{2,1,0:T(8,128)} fusion(bf16[2048,512]{1,0:T(8,128)(2,1)} %collective-permute-done.17, bf16[1024,2048]{1,0:T(8,128)(2,1)} %bitcast.18, bf16[1024,512]{1,0:T(8,128)(2,1)} %get-tuple-element.125), kind=kOutput, calls=%fused_computation.18 | convolution fusion | flops 2149580800 | bytes 11534336 | tf_op jit(solution)/shard_map/dot_general | solution.py:23
  496.9 27.0 %all-to-all-done.5 = bf16[64,208,128]{2,1,0:T(8,128)(2,1)} async-done(((bf16[64,208,128]{2,1,0:T(8,128)(2,1)}), bf16[64,208,128]{2,1,0:T(8,128)(2,1)}, u32[]{:S(2)}, u32[]{:S(2)}) %all-to-all-start.5) | async-done | bytes 3407904 | tf_op jit(solution)/shard_map/all_to_all | solution.py:31
  523.9 8.0 %all-to-all-start.7 = ((bf16[64,88,128]{2,1,0:T(8,128)(2,1)}), bf16[64,88,128]{2,1,0:T(8,128)(2,1)}, u32[]{:S(2)}, u32[]{:S(2)}) async-start(bf16[64,88,128]{2,1,0:T(8,128)(2,1)} %fusion.24), calls=%async_computation.7 | async-start | bytes 2883584 | tf_op jit(solution)/shard_map/all_to_all | solution.py:31
  541.9 12.0 %all-to-all-done.7 = bf16[64,88,128]{2,1,0:T(8,128)(2,1)} async-done(((bf16[64,88,128]{2,1,0:T(8,128)(2,1)}), bf16[64,88,128]{2,1,0:T(8,128)(2,1)}, u32[]{:S(2)}, u32[]{:S(2)}) %all-to-all-start.7) | async-done | bytes 1441824 | tf_op jit(solution)/shard_map/all_to_all | solution.py:31
  (421 shorter events, 218.8 us)
Async XLA Ops:
  33.5 4.7 collective-permute-start.2
  45.6 66.6 %all-to-all-start = ((bf16[64,16,2048]{2,1,0:T(8,128)(2,1)}), bf16[64,16,2048]{2,1,0:T(8,128)(2,1)}, u32[]{:S(2)}, u32[]{:S(2)}) async-start(bf16[64,16,2048]{2,1,0:T(8,128)(2,1)} %bitcast.293), calls=%async_computation | async-start | bytes 8388608 | tf_op jit(solution)/shard_map/all_to_all | solution.py:31
  112.2 59.9 %all-to-all-start.2 = ((bf16[64,16,2048]{2,1,0:T(8,128)(2,1)}), bf16[64,16,2048]{2,1,0:T(8,128)(2,1)}, u32[]{:S(2)}, u32[]{:S(2)}) async-start(bf16[64,16,2048]{2,1,0:T(8,128)(2,1)} %bitcast.292), calls=%async_computation.2 | async-start | bytes 8388608 | tf_op jit(solution)/shard_map/all_to_all | solution.py:31
  118.7 76.4 %collective-permute-start.5 = (bf16[512,2048]{1,0:T(8,128)(2,1)}, bf16[512,2048]{1,0:T(8,128)(2,1)}, u32[]{:S(2)}, u32[]{:S(2)}) collective-permute-start(bf16[512,2048]{1,0:T(8,128)(2,1)} %bitcast.365), channel_id=1, source_target_pairs={{0,1},{1,0},{2,3},{3,2},{4,5},{5,4},{6,7},{7,6},{8,9},{9,8},{10,11... | collective-permute-start | bytes 6291464 | tf_op jit(solution)/shard_map/ppermute | solution.py:15
  118.8 68.1 %collective-permute-start.4 = (bf16[2048,512]{1,0:T(8,128)(2,1)}, bf16[2048,512]{1,0:T(8,128)(2,1)}, u32[]{:S(2)}, u32[]{:S(2)}) collective-permute-start(bf16[2048,512]{1,0:T(8,128)(2,1)} %bitcast.366), channel_id=1, source_target_pairs={{0,1},{1,0},{2,3},{3,2},{4,5},{5,4},{6,7},{7,6},{8,9},{9,8},{10,11... | collective-permute-start | bytes 6291464 | tf_op jit(solution)/shard_map/ppermute | solution.py:15
  119.3 81.7 %collective-permute-start.3 = (bf16[2048,512]{1,0:T(8,128)(2,1)}, bf16[2048,512]{1,0:T(8,128)(2,1)}, u32[]{:S(2)}, u32[]{:S(2)}) collective-permute-start(bf16[2048,512]{1,0:T(8,128)(2,1)} %bitcast.367), channel_id=1, source_target_pairs={{0,1},{1,0},{2,3},{3,2},{4,5},{5,4},{6,7},{7,6},{8,9},{9,8},{10,11... | collective-permute-start | bytes 6291464 | tf_op jit(solution)/shard_map/ppermute | solution.py:15
  215.0 58.4 %all-to-all-start.1 = ((bf16[64,16,2048]{2,1,0:T(8,128)(2,1)}), bf16[64,16,2048]{2,1,0:T(8,128)(2,1)}, u32[]{:S(2)}, u32[]{:S(2)}) async-start(bf16[64,16,2048]{2,1,0:T(8,128)(2,1)} %bitcast.297), calls=%async_computation.1 | async-start | bytes 8388608 | tf_op jit(solution)/shard_map/all_to_all | solution.py:31
  222.1 107.7 %all-gather.5.cloned.1.call-start = ((), (), s32[]{:S(2)}) async-start(), calls=%async_computation.8 | async-start | bytes 2621440 | tf_op jit(solution)/shard_map/all_gather | solution.py:132
  273.4 83.2 %all-to-all-start.3 = ((bf16[64,16,2048]{2,1,0:T(8,128)(2,1)}), bf16[64,16,2048]{2,1,0:T(8,128)(2,1)}, u32[]{:S(2)}, u32[]{:S(2)}) async-start(bf16[64,16,2048]{2,1,0:T(8,128)(2,1)} %bitcast.294), calls=%async_computation.3 | async-start | bytes 8388608 | tf_op jit(solution)/shard_map/all_to_all | solution.py:31
  280.9 181.0 %all-gather.7.cloned.1.call-start = ((), (), s32[]{:S(2)}) async-start(), calls=%async_computation.9 | async-start | bytes 2621440 | tf_op jit(solution)/shard_map/all_gather | solution.py:254
  333.8 115.5 %collective-permute-start.13 = (bf16[4,128,2048]{1,2,0:T(8,128)(2,1)}, bf16[4,128,2048]{1,2,0:T(8,128)(2,1)}, u32[]{:S(2)}, u32[]{:S(2)}) collective-permute-start(bf16[4,128,2048]{1,2,0:T(8,128)(2,1)} %copy.306), channel_id=1, source_target_pairs={{0,1},{1,0},{2,3},{3,2},{4,5},{5,4},{6,7},{7,6},{8,9},{9,8},{10,11... | collective-permute-start | bytes 6291464 | tf_op jit(solution)/shard_map/ppermute | solution.py:15
  339.8 33.9 %collective-permute-start.19 = (bf16[512,2048]{1,0:T(8,128)(2,1)}, bf16[512,2048]{1,0:T(8,128)(2,1)S(1)}, u32[]{:S(2)}, u32[]{:S(2)}) collective-permute-start(bf16[512,2048]{1,0:T(8,128)(2,1)} %convolution_convert_fusion.2), channel_id=1, source_target_pairs={{0,1},{1,0},{2,3},{3,2},{4,5},{5,4},{6,7},{7,6},{8,9},{9,8},{10,11... | collective-permute-start | bytes 6291464 | tf_op jit(solution)/shard_map/ppermute | solution.py:15
  346.3 80.6 %collective-permute-start.18 = (bf16[2048,512]{1,0:T(8,128)(2,1)}, bf16[2048,512]{1,0:T(8,128)(2,1)}, u32[]{:S(2)}, u32[]{:S(2)}) collective-permute-start(bf16[2048,512]{1,0:T(8,128)(2,1)} %convolution_convert_fusion.3), channel_id=1, source_target_pairs={{0,1},{1,0},{2,3},{3,2},{4,5},{5,4},{6,7},{7,6},{8,9},{9,8},{10,11... | collective-permute-start | bytes 6291464 | tf_op jit(solution)/shard_map/ppermute | solution.py:15
  352.5 126.4 %collective-permute-start.17 = (bf16[2048,512]{1,0:T(8,128)(2,1)}, bf16[2048,512]{1,0:T(8,128)(2,1)}, u32[]{:S(2)}, u32[]{:S(2)}) collective-permute-start(bf16[2048,512]{1,0:T(8,128)(2,1)} %convolution_convert_fusion.4), channel_id=1, source_target_pairs={{0,1},{1,0},{2,3},{3,2},{4,5},{5,4},{6,7},{7,6},{8,9},{9,8},{10,11... | collective-permute-start | bytes 6291464 | tf_op jit(solution)/shard_map/ppermute | solution.py:15
  360.3 8.9 %collective-permute-start.8 = (f32[128,2048]{1,0:T(8,128)S(1)}, f32[128,2048]{1,0:T(8,128)S(1)}, u32[]{:S(2)}, u32[]{:S(2)}) collective-permute-start(f32[128,2048]{1,0:T(8,128)S(1)} %slice.389), channel_id=1, source_target_pairs={{0,1},{1,0},{2,3},{3,2},{4,5},{5,4},{6,7},{7,6},{8,9},{9,8},{10,11... | collective-permute-start | bytes 3145736 | tf_op jit(solution)/shard_map/ppermute | solution.py:15
  373.1 7.5 %collective-permute-start.10 = (bf16[128,2048]{1,0:T(8,128)(2,1)}, bf16[128,2048]{1,0:T(8,128)(2,1)}, u32[]{:S(2)}, u32[]{:S(2)}) collective-permute-start(bf16[128,2048]{1,0:T(8,128)(2,1)} %get-tuple-element.115), channel_id=1, source_target_pairs={{0,1},{1,0},{2,3},{3,2},{4,5},{5,4},{6,7},{7,6},{8,9},{9,8},{10,11... | collective-permute-start | bytes 1572872 | tf_op jit(solution)/shard_map/ppermute | solution.py:15
  397.8 6.3 %collective-permute-start.11 = (f32[2,256]{1,0:T(2,128)}, f32[2,256]{1,0:T(2,128)}, u32[]{:S(2)}, u32[]{:S(2)}) collective-permute-start(f32[2,256]{1,0:T(2,128)} %pad_maximum_fusion.8), channel_id=1, source_target_pairs={{0,1},{1,0},{2,3},{3,2},{4,5},{5,4},{6,7},{7,6},{8,9},{9,8},{10,11... | collective-permute-start | bytes 6152 | tf_op jit(solution)/shard_map/ppermute | solution.py:15
  416.8 6.8 %collective-permute-start.12 = (f32[128,2048]{1,0:T(8,128)}, f32[128,2048]{1,0:T(8,128)}, u32[]{:S(2)}, u32[]{:S(2)}) collective-permute-start(f32[128,2048]{1,0:T(8,128)} %slice.403), channel_id=1, source_target_pairs={{0,1},{1,0},{2,3},{3,2},{4,5},{5,4},{6,7},{7,6},{8,9},{9,8},{10,11... | collective-permute-start | bytes 3145736 | tf_op jit(solution)/shard_map/ppermute | solution.py:15
  419.1 25.9 %all-to-all-start.4 = ((bf16[4,256,768]{2,1,0:T(8,128)(2,1)}), bf16[4,256,768]{2,1,0:T(8,128)(2,1)}, u32[]{:S(2)}, u32[]{:S(2)}) async-start(bf16[4,256,768]{2,1,0:T(8,128)(2,1)} %pad_maximum_fusion), calls=%async_computation.4 | async-start | bytes 3145728 | tf_op jit(solution)/shard_map/all_to_all | solution.py:31
  426.8 13.2 %collective-permute-start.14 = (f32[64,16]{1,0:T(8,128)}, f32[64,16]{1,0:T(8,128)}, u32[]{:S(2)}, u32[]{:S(2)}) collective-permute-start(f32[64,16]{1,0:T(8,128)} %bitcast.57), channel_id=1, source_target_pairs={{0,1},{1,0},{2,3},{3,2},{4,5},{5,4},{6,7},{7,6},{8,9},{9,8},{10,11... | collective-permute-start | bytes 12296 | tf_op jit(solution)/shard_map/ppermute | solution.py:15
  445.0 20.8 %all-to-all-start.6 = ((bf16[4,256,256]{2,1,0:T(8,128)(2,1)}), bf16[4,256,256]{2,1,0:T(8,128)(2,1)}, u32[]{:S(2)}, u32[]{:S(2)}) async-start(bf16[4,256,256]{2,1,0:T(8,128)(2,1)} %pad_maximum_fusion.4), calls=%async_computation.6 | async-start | bytes 1048576 | tf_op jit(solution)/shard_map/all_to_all | solution.py:31
  465.8 25.5 %collective-permute-start.15 = (bf16[4,128,2048]{1,2,0:T(8,128)(2,1)}, bf16[4,128,2048]{1,2,0:T(8,128)(2,1)}, u32[]{:S(2)}, u32[]{:S(2)}) collective-permute-start(bf16[4,128,2048]{1,2,0:T(8,128)(2,1)} %copy.320), channel_id=1, source_target_pairs={{0,1},{1,0},{2,3},{3,2},{4,5},{5,4},{6,7},{7,6},{8,9},{9,8},{10,11... | collective-permute-start | bytes 6291464 | tf_op jit(solution)/shard_map/ppermute | solution.py:15
  465.8 58.1 %all-to-all-start.5 = ((bf16[64,208,128]{2,1,0:T(8,128)(2,1)}), bf16[64,208,128]{2,1,0:T(8,128)(2,1)}, u32[]{:S(2)}, u32[]{:S(2)}) async-start(bf16[64,208,128]{2,1,0:T(8,128)(2,1)} %pad_dynamic-update-slice_fusion), calls=%async_computation.5 | async-start | bytes 6815744 | tf_op jit(solution)/shard_map/all_to_all | solution.py:31
  523.9 29.9 %all-to-all-start.7 = ((bf16[64,88,128]{2,1,0:T(8,128)(2,1)}), bf16[64,88,128]{2,1,0:T(8,128)(2,1)}, u32[]{:S(2)}, u32[]{:S(2)}) async-start(bf16[64,88,128]{2,1,0:T(8,128)(2,1)} %fusion.24), calls=%async_computation.7 | async-start | bytes 2883584 | tf_op jit(solution)/shard_map/all_to_all | solution.py:31
  (96 other events, 1072.3 us)
Sparse Core Ops, SparseCore 0:
  225.5 104.1 all-gather.4
  380.8 33.1 all-gather.6

commit v2 on v1

v2 whole, which is shorter than its diff:
```python
import jax
import jax.numpy as jnp
from jax import lax
from jax.experimental import pallas as pl
from jax.experimental.pallas import tpu as pltpu
from jax.sharding import Mesh, PartitionSpec as P

norm_eps = 1e-05
rope_base = 10000.0
mask_fill = -1e30
bf16 = jnp.bfloat16
f32 = jnp.float32
rows_of_chips = ("z", "x", "y")


def swap(value):
    return lax.ppermute(value, "tp", [(0, 1), (1, 0)])


def dot(left, right):
    return lax.dot_general(left, right, (((1,), (0,)), ((), ())), preferred_element_type=f32)


def dot_rows(left, right):
    return lax.dot_general(left, right, (((0,), (0,)), ((), ())), preferred_element_type=f32)


def dot_cols(left, right):
    return lax.dot_general(left, right, (((1,), (1,)), ((), ())), preferred_element_type=f32)


def all_to_all(value, axes):
    return lax.all_to_all(value, axes, split_axis=0, concat_axis=0, tiled=True)


def rms_scale(values):
    return lax.rsqrt(jnp.mean(values * values, axis=-1, keepdims=True) + norm_eps)


def halves(value):
    high = value.astype(bf16)
    return high, (value - high.astype(f32)).astype(bf16)


def rope_angles(positions, head_dim):
    half_dim = head_dim // 2
    exponent = jnp.arange(half_dim, dtype=f32) * (2.0 / head_dim)
    inverse = jnp.power(f32(rope_base), -exponent)
    angles = positions.astype(f32)[:, None] * inverse[None, :]
    return jnp.cos(angles), jnp.sin(angles)


lanes = 128
vmem_bytes = 56 * 1024 * 1024
cheap = 64


def params():
    return pltpu.CompilerParams(vmem_limit_bytes=vmem_bytes)


def turn(value, cosine, sine):
    return value * cosine + pltpu.roll(value, value.shape[1] // 2, 1) * sine


def attention_forward_body(
    scale,
    query_ref,
    key_ref,
    value_ref,
    query_gain_ref,
    key_gain_ref,
    query_scale_ref,
    key_scale_ref,
    cosine_ref,
    sine_ref,
    bias_ref,
    q_rot_ref,
    k_rot_ref,
    probs_ref,
    mixed_ref,
):
    cosine, sine = cosine_ref[...], sine_ref[...]
    query = query_ref[...] * query_scale_ref[...] * query_gain_ref[...]
    key = key_ref[...] * key_scale_ref[...] * key_gain_ref[...]
    q_rot = turn(query, cosine, sine).astype(bf16)
    k_rot = turn(key, cosine, sine).astype(bf16)
    q_rot_ref[...] = q_rot
    k_rot_ref[...] = k_rot
    scores = dot_cols(q_rot, k_rot) * scale + bias_ref[...]
    grown = jnp.exp(scores - jnp.max(scores, axis=1, keepdims=True))
    probs = grown / jnp.sum(grown, axis=1, keepdims=True)
    probs_ref[...] = probs
    mixed_ref[...] = dot(probs.astype(bf16), value_ref[...]).astype(bf16)


def attention_forward(
    queries, keys, values, query_gain, key_gain, query_scale, key_scale, cosine, sine, bias, heads
):
    seq_len, width = queries.shape
    head = width // heads
    column = pl.BlockSpec((seq_len, head), lambda h: (0, h))
    gain = pl.BlockSpec((1, head), lambda h: (0, h))

    def whole(array):
        return pl.BlockSpec(array.shape, lambda h: (0, 0))

    return pl.pallas_call(
        lambda *refs: attention_forward_body(head**-0.5, *refs),
        grid=(heads,),
        in_specs=[column, column, column, gain, gain]
        + [whole(a) for a in (query_scale, key_scale, cosine, sine, bias)],
        out_specs=[
            column,
            column,
            pl.BlockSpec((None, seq_len, seq_len), lambda h: (h, 0, 0)),
            column,
        ],
        out_shape=[
            jax.ShapeDtypeStruct((seq_len, width), bf16),
            jax.ShapeDtypeStruct((seq_len, width), bf16),
            jax.ShapeDtypeStruct((heads, seq_len, seq_len), f32),
            jax.ShapeDtypeStruct((seq_len, width), bf16),
        ],
        compiler_params=params(),
        cost_estimate=pl.CostEstimate(
            flops=4 * seq_len * seq_len * width,
            transcendentals=heads * seq_len * seq_len,
            bytes_accessed=seq_len * width * 16 + heads * seq_len * seq_len * 4,
        ),
        name="attention_forward",
    )(queries, keys, values, query_gain, key_gain, query_scale, key_scale, cosine, sine, bias)


def attention_backward_body(
    scale,
    hidden_ref,
    w_out_ref,
    value_ref,
    q_rot_ref,
    k_rot_ref,
    probs_ref,
    query_ref,
    key_ref,
    query_gain_ref,
    key_gain_ref,
    query_scale_ref,
    key_scale_ref,
    cosine_ref,
    sine_ref,
    value_grad_ref,
    query_part_ref,
    key_part_ref,
    query_gain_grad_ref,
    key_gain_grad_ref,
    query_inner_ref,
    key_inner_ref,
):
    cosine, sine = cosine_ref[...], sine_ref[...]
    grad_mixed = dot_cols(hidden_ref[...], w_out_ref[...]).astype(bf16)
    probs = probs_ref[...]
    grad_probs = dot_cols(grad_mixed, value_ref[...])
    inner = jnp.sum(probs * grad_probs, axis=1, keepdims=True)
    grad_scores = (probs * (grad_probs - inner)).astype(bf16)
    value_grad_ref[...] = dot_rows(probs.astype(bf16), grad_mixed).astype(bf16)
    first = pl.program_id(0) == 0
    for grad_rot, raw_ref, gain_ref, scale_ref, part_ref, gain_grad_ref, inner_ref in (
        (
            dot(grad_scores, k_rot_ref[...]),
            query_ref,
            query_gain_ref,
            query_scale_ref,
            query_part_ref,
            query_gain_grad_ref,
            query_inner_ref,
        ),
        (
            dot_rows(grad_scores, q_rot_ref[...]),
            key_ref,
            key_gain_ref,
            key_scale_ref,
            key_part_ref,
            key_gain_grad_ref,
            key_inner_ref,
        ),
    ):
        grad_normed = turn(grad_rot * scale, cosine, -sine)
        raw = raw_ref[...]
        gain_grad_ref[...] = jnp.sum(raw * scale_ref[...] * grad_normed, axis=0, keepdims=True)
        weighted = grad_normed * gain_ref[...]
        part_ref[...] = weighted
        row_inner = jnp.sum(raw * weighted, axis=1, keepdims=True)

        @pl.when(first)
        def _():
            inner_ref[...] = row_inner

        @pl.when(jnp.logical_not(first))
        def _():
            inner_ref[...] += row_inner


def attention_backward(
    hidden_low,
    w_out,
    values,
    q_rot,
    k_rot,
    probs,
    queries,
    keys,
    query_gain,
    key_gain,
    query_scale,
    key_scale,
    cosine,
    sine,
    heads,
):
    seq_len, width = queries.shape
    head = width // heads
    column = pl.BlockSpec((seq_len, head), lambda h: (0, h))
    gain = pl.BlockSpec((1, head), lambda h: (0, h))

    def whole(array):
        return pl.BlockSpec(array.shape, lambda h: (0, 0))

    full = jax.ShapeDtypeStruct((seq_len, width), f32)
    line = jax.ShapeDtypeStruct((1, width), f32)
    sums = jax.ShapeDtypeStruct((seq_len, 1), f32)
    return pl.pallas_call(
        lambda *refs: attention_backward_body(head**-0.5, *refs),
        grid=(heads,),
        in_specs=[
            whole(hidden_low),
            pl.BlockSpec((head, w_out.shape[1]), lambda h: (h, 0)),
            column,
            column,
            column,
            pl.BlockSpec((None, seq_len, seq_len), lambda h: (h, 0, 0)),
            column,
            column,
            gain,
            gain,
        ]
        + [whole(a) for a in (query_scale, key_scale, cosine, sine)],
        out_specs=[column, column, column, gain, gain, whole(sums), whole(sums)],
        out_shape=[
            jax.ShapeDtypeStruct((seq_len, width), bf16),
            full,
            full,
            line,
            line,
            sums,
            sums,
        ],
        compiler_params=params(),
        cost_estimate=pl.CostEstimate(
            flops=10 * seq_len * seq_len * width + 2 * seq_len * width * w_out.shape[1],
            transcendentals=0,
            bytes_accessed=seq_len * width * 28
            + heads * seq_len * seq_len * 4
            + 2 * w_out.size
            + 2 * hidden_low.size,
        ),
        name="attention_backward",
    )(
        hidden_low,
        w_out,
        values,
        q_rot,
        k_rot,
        probs,
        queries,
        keys,
        query_gain,
        key_gain,
        query_scale,
        key_scale,
        cosine,
        sine,
    )


def projection_grads_body(
    query_part_ref,
    key_part_ref,
    query_ref,
    key_ref,
    value_grad_ref,
    query_scale_ref,
    key_scale_ref,
    query_inner_ref,
    key_inner_ref,
    query_grad_ref,
    key_grad_ref,
    stack_ref,
):
    size = query_ref.shape[1]
    for k, (part_ref, raw_ref, scale_ref, inner_ref, grad_ref) in enumerate(
        (
            (query_part_ref, query_ref, query_scale_ref, query_inner_ref, query_grad_ref),
            (key_part_ref, key_ref, key_scale_ref, key_inner_ref, key_grad_ref),
        )
    ):
        scale = scale_ref[...]
        grad = scale * part_ref[...] - raw_ref[...] * (scale * scale * scale * inner_ref[...])
        grad = grad.astype(bf16)
        grad_ref[...] = grad
        stack_ref[:, k * size : (k + 1) * size] = grad
    stack_ref[:, 2 * size :] = value_grad_ref[...]


def projection_grads(
    query_part, key_part, queries, keys, value_grad, query_scale, key_scale, inners, planes
):
    seq_len, width = queries.shape
    size = width // planes
    column = pl.BlockSpec((seq_len, size), lambda k: (0, k))
    sums = pl.BlockSpec((seq_len, 1), lambda k: (0, 0))
    grads = jax.ShapeDtypeStruct((seq_len, width), bf16)
    return pl.pallas_call(
        projection_grads_body,
        grid=(planes,),
        in_specs=[column] * 5 + [sums] * 4,
        out_specs=[
            column,
            column,
            pl.BlockSpec((None, seq_len, 3 * size), lambda k: (k, 0, 0)),
        ],
        out_shape=[grads, grads, jax.ShapeDtypeStruct((planes, seq_len, 3 * size), bf16)],
        compiler_params=params(),
        cost_estimate=pl.CostEstimate(
            flops=10 * seq_len * width, transcendentals=0, bytes_accessed=28 * seq_len * width
        ),
        name="projection_grads",
    )(query_part, key_part, queries, keys, value_grad, query_scale, key_scale, *inners)


def expert_forward_body(
    rows_ref,
    gate_own_ref,
    gate_other_ref,
    up_own_ref,
    up_other_ref,
    down_own_ref,
    down_other_ref,
    gate_act_own_ref,
    gate_act_other_ref,
    up_act_own_ref,
    up_act_other_ref,
    out_ref,
    total_ref,
):
    step = pl.program_id(0)
    last = pl.num_programs(0) - 1
    count = rows_ref.shape[0]
    size = min(256, count)
    for start in range(0, count, size):
        here = pl.ds(start, size)
        rows = rows_ref[here, :]
        total = None
        for gate_ref, up_ref, down_ref, gate_act_ref, up_act_ref in (
            (gate_own_ref, up_own_ref, down_own_ref, gate_act_own_ref, up_act_own_ref),
            (gate_other_ref, up_other_ref, down_other_ref, gate_act_other_ref, up_act_other_ref),
        ):
            gate = dot(rows, gate_ref[...])
            up = dot(rows, up_ref[...])
            gate_act_ref[here, :] = gate
            up_act_ref[here, :] = up
            inner = (gate * jax.nn.sigmoid(gate) * up).astype(bf16)
            part = dot(inner, down_ref[...])
            total = part if total is None else total + part

        @pl.when(step == 0)
        def _():
            total_ref[here, :] = total

        @pl.when((step > 0) & (step < last))
        def _():
            total_ref[here, :] += total

        @pl.when(step == last)
        def _():
            out_ref[here, :] = (total_ref[here, :] + total).astype(bf16)


def expert_forward(rows, gates, ups, downs):
    count, width = rows.shape
    units = gates[0].shape[1]
    steps = 2
    size = units // steps
    into = pl.BlockSpec((width, size), lambda k: (0, k))
    back = pl.BlockSpec((size, width), lambda k: (k, 0))
    acts = pl.BlockSpec((count, size), lambda k: (0, k))
    act = jax.ShapeDtypeStruct((count, units), f32)
    whole = pl.BlockSpec((count, width), lambda k: (0, 0))
    return pl.pallas_call(
        expert_forward_body,
        grid=(steps,),
        in_specs=[whole] + [into] * 4 + [back] * 2,
        out_specs=[acts] * 4 + [whole],
        out_shape=[act] * 4 + [jax.ShapeDtypeStruct((count, width), bf16)],
        scratch_shapes=[pltpu.VMEM((count, width), f32)],
        compiler_params=params(),
        cost_estimate=pl.CostEstimate(
            flops=12 * count * width * units,
            transcendentals=2 * count * units,
            bytes_accessed=count * width * 4 + 12 * width * units + 16 * count * units,
        ),
        name="expert_forward",
    )(rows, *gates, *ups, *downs)


def weight_parcel_body(left_ref, right_ref, extra_ref, out_ref):
    chips, height, _ = out_ref.shape
    product = dot_rows(left_ref[...], right_ref[...]).astype(bf16)
    rows = product.shape[0] // chips
    blocks = product.shape[1] // lanes
    for k in range(blocks):
        piece = product[:, k * lanes : (k + 1) * lanes].reshape(chips, rows, lanes)
        out_ref[:, k * rows : (k + 1) * rows, :] = piece
    out_ref[:, blocks * rows :, :] = extra_ref[...]


def weight_parcel(left, right, extra, steps):
    chips, extra_rows, _ = extra.shape
    tokens, width = left.shape
    columns = right.shape[1]
    rows = width // chips
    height = rows * (columns // lanes) + extra_rows
    return pl.pallas_call(
        weight_parcel_body,
        grid=(steps,),
        in_specs=[
            pl.BlockSpec((tokens, width // steps), lambda k: (0, k)),
            pl.BlockSpec((tokens, columns), lambda k: (0, 0)),
            pl.BlockSpec((chips // steps, extra_rows, lanes), lambda k: (k, 0, 0)),
        ],
        out_specs=pl.BlockSpec((chips // steps, height, lanes), lambda k: (k, 0, 0)),
        out_shape=jax.ShapeDtypeStruct((chips, height, lanes), bf16),
        compiler_params=params(),
        cost_estimate=pl.CostEstimate(
            flops=2 * tokens * width * columns,
            transcendentals=0,
            bytes_accessed=2 * (left.size + right.size + chips * height * lanes),
        ),
        name="weight_parcel",
    )(left, right, extra)


def expert_weight_grads_body(rows_ref, slot_grad_ref, inner_ref, gate_ref, up_ref, *refs):
    grads = (
        dot_rows(rows_ref[...], gate_ref[...]),
        dot_rows(rows_ref[...], up_ref[...]),
        dot_rows(inner_ref[...], slot_grad_ref[...]),
    )
    others, outs = refs[:-3], refs[-3:]
    for k, (grad, out_ref) in enumerate(zip(grads, outs)):
        if others:
            grad = grad + others[k][...].astype(f32)
        out_ref[...] = grad.astype(out_ref.dtype)


def expert_weight_grads(rows, slot_grad, inner, gate_grad, up_grad, others, kind):
    count, width = rows.shape
    units = inner.shape[1]
    steps = 4
    size = width // steps
    wide = pl.BlockSpec((count, size), lambda k: (0, k))
    narrow = pl.BlockSpec((count, units), lambda k: (0, 0))
    into = pl.BlockSpec((size, units), lambda k: (k, 0))
    back = pl.BlockSpec((units, size), lambda k: (0, k))
    return pl.pallas_call(
        expert_weight_grads_body,
        grid=(steps,),
        in_specs=[wide, wide, narrow, narrow, narrow] + [into, into, back][: len(others)],
        out_specs=[into, into, back],
        out_shape=[
            jax.ShapeDtypeStruct((width, units), kind),
            jax.ShapeDtypeStruct((width, units), kind),
            jax.ShapeDtypeStruct((units, width), kind),
        ],
        compiler_params=params(),
        cost_estimate=pl.CostEstimate(
            flops=6 * count * width * units // cheap,
            transcendentals=0,
            bytes_accessed=4 * count * width // cheap,
        ),
        name="expert_weight_grads",
    )(rows, slot_grad, inner, gate_grad, up_grad, *others)


def normed_grad_body(*refs):
    *pairs, out_ref = refs
    total = None
    for grad_ref, w_ref in zip(pairs[:3], pairs[3:]):
        part = dot_cols(grad_ref[...], w_ref[...])
        total = part if total is None else total + part
    first = pl.program_id(0) == 0

    @pl.when(first)
    def _():
        out_ref[...] = total

    @pl.when(jnp.logical_not(first))
    def _():
        out_ref[...] += total


def normed_grad_of(grads, weights, steps):
    seq_len, width = grads[0].shape
    size = width // steps
    full = weights[0].shape[0]
    return pl.pallas_call(
        normed_grad_body,
        grid=(steps,),
        in_specs=[pl.BlockSpec((seq_len, size), lambda k: (0, k))] * 3
        + [pl.BlockSpec((full, size), lambda k: (0, k))] * 3,
        out_specs=pl.BlockSpec((seq_len, full), lambda k: (0, 0)),
        out_shape=jax.ShapeDtypeStruct((seq_len, full), f32),
        compiler_params=params(),
        cost_estimate=pl.CostEstimate(
            flops=6 * seq_len * width * full // cheap,
            transcendentals=0,
            bytes_accessed=6 * width * full // cheap,
        ),
        name="normed_grad",
    )(*grads, *weights)


def local(
    residual_in,
    routes,
    segment_ids,
    gain_attn,
    w_query,
    w_key,
    w_value,
    gain_query,
    gain_key,
    w_out,
    gain_moe,
    w_router,
    w_gate,
    w_up,
    w_down,
    cotangent,
):
    core = lax.axis_index("tp")
    planes = lax.axis_size("z")
    chips = lax.axis_size(rows_of_chips)
    chip = lax.axis_index(rows_of_chips)
    own_rows, width = residual_in.shape
    seq_len, top_count = routes.shape
    local_width = w_query.shape[1]
    local_heads, head_dim = gain_query.shape
    full_width = 2 * local_width
    experts = chips
    capacity = seq_len * top_count // experts
    own_slots = capacity // 2
    score_scale = head_dim ** (-0.5)
    quarter = local_width // planes
    out_rows = width // chips

    def own_first(value):
        return jnp.where(
            core == 0, value, jnp.concatenate([value[own_rows:], value[:own_rows]], axis=0)
        )

    def other_order(value):
        return jnp.concatenate([value[own_rows:], value[:own_rows]], axis=0)

    place = own_first(jnp.arange(seq_len, dtype=jnp.int32))
    seg = own_first(segment_ids[0])
    route = own_first(routes)
    same_doc = seg[:, None] == seg[None, :]
    position = place - jnp.min(jnp.where(same_doc, place[None, :], seq_len), axis=1)
    cosine, sine = rope_angles(position, head_dim)
    cosine = jnp.concatenate([cosine, cosine], axis=1)
    sine = jnp.concatenate([-sine, sine], axis=1)
    bias = jnp.where(same_doc & (place[None, :] <= place[:, None]), 0.0, mask_fill)

    hits = jnp.any(
        route[:, :, None] == jnp.arange(experts, dtype=jnp.int32)[None, None, :], axis=1
    )
    before = (place[None, :] < place[:, None]).astype(bf16)
    rank = dot(before, hits.astype(bf16)).astype(jnp.int32)
    rank = jnp.where(hits, rank, -1)
    counts = jnp.sum(hits.astype(f32), axis=0)
    slot_number = core * own_slots + jnp.arange(own_slots, dtype=jnp.int32)
    pick = (rank.T[:, None, :] == slot_number[None, :, None]).astype(bf16)
    pick = pick.reshape(experts * own_slots, seq_len)

    cot = jnp.concatenate([cotangent, swap(cotangent)], axis=0)
    cot_slots = dot(pick, cot).astype(bf16).reshape(experts, own_slots, width)
    cot_arrived = all_to_all(cot_slots, rows_of_chips).reshape(experts * own_slots, width)

    whole_in = jnp.concatenate([residual_in, swap(residual_in)], axis=0).astype(f32)
    scale_attn = rms_scale(whole_in)
    normed = (whole_in * scale_attn * gain_attn).astype(bf16)
    normed_own = normed[:own_rows]
    normed_planes = lax.all_gather(normed_own, "z", axis=0, tiled=False)
    queries = dot(normed, w_query)
    key_proj = dot(normed, w_key)
    values = dot(normed, w_value).astype(bf16)
    squares = jnp.stack([jnp.sum(queries * queries, axis=1), jnp.sum(key_proj * key_proj, axis=1)])
    squares = squares + other_order(swap(squares).T).T
    query_scale = lax.rsqrt(squares[0] / full_width + norm_eps)[:, None]
    key_scale = lax.rsqrt(squares[1] / full_width + norm_eps)[:, None]
    query_gain = gain_query.reshape(1, local_width)
    key_gain = gain_key.reshape(1, local_width)
    q_rot, k_rot, probs, mixed = attention_forward(
        queries,
        key_proj,
        values,
        query_gain,
        key_gain,
        query_scale,
        key_scale,
        cosine,
        sine,
        bias,
        local_heads,
    )
    mixed_planes = lax.all_gather(mixed, "z", axis=0, tiled=False)
    branch = dot(mixed, w_out)
    branch = branch + other_order(swap(branch))
    hidden = whole_in + branch
    scale_moe = rms_scale(hidden)
    normed_moe = (hidden * scale_moe * gain_moe).astype(bf16)

    moe_slots = dot(pick, normed_moe).astype(bf16).reshape(experts, own_slots, width)
    moe_slots, cot_arrived = lax.optimization_barrier((moe_slots, cot_arrived))
    arrived = all_to_all(moe_slots, rows_of_chips).reshape(experts * own_slots, width)
    router_probs = jax.nn.softmax(dot(normed_moe, w_router), axis=-1)

    gate_parts = (w_gate[0], swap(w_gate[0]))
    up_parts = (w_up[0], swap(w_up[0]))
    down_parts = (w_down[0], swap(w_down[0]))
    slot_probs = jax.nn.softmax(dot(arrived, w_router), axis=-1)
    own_expert = jnp.arange(experts, dtype=jnp.int32) == chip
    slot_weight = jnp.sum(jnp.where(own_expert[None, :], slot_probs, 0.0), axis=1, keepdims=True)
    slot_grad = (slot_weight * cot_arrived.astype(f32)).astype(bf16)
    *acts, slot_out = expert_forward(arrived, gate_parts, up_parts, down_parts)
    slot_out, normed_planes, mixed_planes = lax.optimization_barrier(
        (slot_out, normed_planes, mixed_planes)
    )
    normed_planes = jnp.concatenate([normed_planes, swap(normed_planes)], axis=1).reshape(
        planes * seq_len, width
    )
    mixed_planes = mixed_planes.reshape(planes * seq_len, local_width)
    returned = all_to_all(
        slot_out.reshape(experts, own_slots, width), rows_of_chips
    ).reshape(experts * own_slots, width)
    part_grads = []
    slot_in_grad = None
    for gate_act, up_act, w_g, w_u, w_d in zip(
        acts[:2], acts[2:], gate_parts, up_parts, down_parts
    ):
        sigmoid_gate = jax.nn.sigmoid(gate_act)
        silu_gate = gate_act * sigmoid_gate
        inner_act = (silu_gate * up_act).astype(bf16)
        inner_grad = dot_cols(slot_grad, w_d)
        up_grad = (inner_grad * silu_gate).astype(bf16)
        gate_grad = (
            inner_grad * up_act * sigmoid_gate * (1.0 + gate_act * (1.0 - sigmoid_gate))
        ).astype(bf16)
        part_in = dot_cols(gate_grad, w_g) + dot_cols(up_grad, w_u)
        slot_in_grad = part_in if slot_in_grad is None else slot_in_grad + part_in
        part_grads.append((inner_act, gate_grad, up_grad))
    slot_in_grad, returned = lax.optimization_barrier((slot_in_grad.astype(bf16), returned))
    grads_back = all_to_all(
        slot_in_grad.reshape(experts, own_slots, width), rows_of_chips
    ).reshape(experts * own_slots, width)
    (inner_own, gate_own, up_own), (inner_other, gate_other, up_other) = part_grads
    others = expert_weight_grads(
        arrived, slot_grad, inner_other, gate_other, up_other, (), bf16
    )
    grads_back, *others = lax.optimization_barrier((grads_back, *others))
    others = [swap(grad) for grad in others]
    grad_w_gate, grad_w_up, grad_w_down = expert_weight_grads(
        arrived, slot_grad, inner_own, gate_own, up_own, others, f32
    )

    pick_pairs = pick.reshape(experts, own_slots, seq_len)
    weighted = pick_pairs.astype(f32) * router_probs.T[:, None, :]
    weight_high, weight_low = halves(weighted.reshape(experts * own_slots, seq_len))
    moe_part = dot_rows(weight_high, returned) + dot_rows(weight_low, returned)
    moe_own = moe_part[:own_rows] + swap(moe_part[own_rows:].astype(bf16)).astype(f32)
    output = (hidden[:own_rows] + moe_own).astype(bf16)
    pair_products = dot_cols(returned, cot).reshape(experts, own_slots, seq_len)
    prob_part = jnp.sum(pair_products * pick_pairs.astype(f32), axis=1).T
    prob_grad = prob_part + other_order(swap(prob_part))
    logit_grad = router_probs * (
        prob_grad - jnp.sum(router_probs * prob_grad, axis=1, keepdims=True)
    )
    logit_high, logit_low = halves(logit_grad)
    router_grad = dot_rows(normed_moe, logit_high) + dot_rows(normed_moe, logit_low)
    moe_in_part = dot_rows(pick, grads_back)
    moe_in_grad = (
        moe_in_part[:own_rows]
        + swap(moe_in_part[own_rows:])
        + dot_cols(logit_high[:own_rows], w_router)
        + dot_cols(logit_low[:own_rows], w_router)
    )
    cot_own = cotangent.astype(f32)
    hidden_own = hidden[:own_rows]
    scale_own = scale_moe[:own_rows]
    weighted_moe = moe_in_grad * gain_moe
    hidden_grad = (
        cot_own
        + scale_own * weighted_moe
        - hidden_own * scale_own**3 * jnp.mean(hidden_own * weighted_moe, axis=1, keepdims=True)
    )
    gain_moe_grad = jnp.sum(hidden_own * scale_own * moe_in_grad, axis=0)
    hidden_low_own = hidden_grad.astype(bf16)
    hidden_low = jnp.concatenate([hidden_low_own, swap(hidden_low_own)], axis=0)

    part = width // planes
    low_planes = all_to_all(
        jnp.stack([hidden_low_own[:, k * part : (k + 1) * part] for k in range(planes)]), "z"
    )

    def for_cores(vector):
        pieces = vector.reshape(chips, 2, -1)
        mine = jnp.where(core == 0, pieces[:, 0], pieces[:, 1])
        others = jnp.where(core == 0, pieces[:, 1], pieces[:, 0])
        return mine + swap(others)

    def small_rows(values):
        high, low = halves(jnp.pad(values, ((0, 0), (0, lanes - values.shape[1]))))
        return jnp.stack([high, low], axis=1)

    router_pieces = router_grad.reshape(chips, 2, out_rows // 2, experts)
    router_mine = jnp.where(core == 0, router_pieces[:, 0], router_pieces[:, 1])
    router_mine = router_mine.reshape(chips, -1, lanes).astype(bf16)
    router_len = router_mine.shape[1]

    (
        value_grad,
        query_part,
        key_part,
        gain_query_grad,
        gain_key_grad,
        query_inner,
        key_inner,
    ) = attention_backward(
        hidden_low,
        w_out,
        values,
        q_rot,
        k_rot,
        probs,
        queries,
        key_proj,
        query_gain,
        key_gain,
        query_scale,
        key_scale,
        cosine,
        sine,
        local_heads,
    )
    query_inner, key_inner, low_planes = lax.optimization_barrier(
        (query_inner, key_inner, low_planes)
    )
    inner = jnp.concatenate([query_inner, key_inner], axis=1)
    inner = (inner + other_order(swap(inner.T).T)) / full_width
    query_grad, key_grad, to_planes = projection_grads(
        query_part,
        key_part,
        queries,
        key_proj,
        value_grad,
        query_scale,
        key_scale,
        (inner[:, :1], inner[:, 1:]),
        planes,
    )

    grads_planes = all_to_all(to_planes, "z").reshape(planes * seq_len, 3 * quarter)
    low_planes = jnp.concatenate([low_planes, swap(low_planes)], axis=1).reshape(
        planes * seq_len, part
    )
    out_grad = dot_rows(low_planes, mixed_planes).astype(bf16)
    out_grad, grads_planes = lax.optimization_barrier((out_grad, grads_planes))
    out_sums = all_to_all(
        out_grad.reshape(chips // planes, out_rows, local_width), rows_of_chips[1:]
    )
    normed_grad = normed_grad_of(
        (query_grad, key_grad, value_grad), (w_query, w_key, w_value), planes
    )
    normed_grad = normed_grad[:own_rows] + swap(normed_grad[own_rows:])
    in_own = whole_in[:own_rows]
    in_scale = scale_attn[:own_rows]
    weighted_attn = normed_grad * gain_attn
    grad_input = (
        hidden_grad
        + in_scale * weighted_attn
        - in_own * in_scale**3 * jnp.mean(in_own * weighted_attn, axis=1, keepdims=True)
    )
    gain_attn_grad = jnp.sum(in_own * in_scale * normed_grad, axis=0)

    def by_lane(vector):
        pieces = vector.reshape(local_heads, chips, head_dim // chips)
        return jnp.swapaxes(pieces, 0, 1).reshape(chips, -1)

    first_small = small_rows(jnp.concatenate([for_cores(gain_moe_grad), counts[:, None]], axis=1))
    last_small = small_rows(
        jnp.concatenate(
            [for_cores(gain_attn_grad), by_lane(gain_query_grad), by_lane(gain_key_grad)], axis=1
        )
    )
    spare = jnp.zeros((chips, -(router_len + 4) % 16, lanes), bf16)
    extra = jnp.concatenate([router_mine, first_small, last_small, spare], axis=1)
    last_parcel = weight_parcel(normed_planes, grads_planes, extra, planes)
    last_parcel, out_sums = lax.optimization_barrier((last_parcel, out_sums))
    last_sums = all_to_all(last_parcel, rows_of_chips).astype(f32)
    last_sums = jnp.sum(last_sums.reshape((planes, chips // planes) + last_sums.shape[1:]), axis=1)

    def matrix_of(blocks):
        pieces = blocks.reshape(planes, -1, out_rows, lanes)
        return jnp.transpose(pieces, (2, 0, 1, 3)).reshape(out_rows, -1)

    block_len = quarter // lanes * out_rows
    grad_w_query, grad_w_key, grad_w_value = (
        matrix_of(last_sums[:, k * block_len : (k + 1) * block_len]) for k in range(3)
    )
    grad_w_out = jnp.sum(out_sums.astype(f32), axis=0).T
    tail = jnp.sum(last_sums[:, 3 * block_len :], axis=0)
    grad_w_router = tail[:router_len].reshape(out_rows // 2, experts)
    first_tail = tail[router_len] + tail[router_len + 1]
    last_tail = tail[router_len + 2] + tail[router_len + 3]
    own_gain = out_rows // 2
    own_lanes = local_heads * head_dim // chips
    lane_shape = (local_heads, head_dim // chips)
    return (
        output,
        grad_input,
        last_tail[:own_gain],
        grad_w_query,
        grad_w_key,
        grad_w_value,
        last_tail[own_gain : own_gain + own_lanes].reshape(lane_shape),
        last_tail[own_gain + own_lanes : own_gain + 2 * own_lanes].reshape(lane_shape),
        grad_w_out,
        first_tail[:own_gain],
        grad_w_router,
        grad_w_gate[None],
        grad_w_up[None],
        grad_w_down[None],
        first_tail[own_gain : own_gain + 1].astype(jnp.int32),
    )


def solution(mesh):
    side = round(mesh.shape["ep"] ** (1 / 3))
    cube = Mesh(mesh.devices.reshape(side, side, side, 2), rows_of_chips + ("tp",))
    ep = rows_of_chips
    both = rows_of_chips + ("tp",)
    in_specs = (
        P(both, None),
        P(ep, None),
        P(ep, None),
        P(),
        P(None, "tp"),
        P(None, "tp"),
        P(None, "tp"),
        P("tp", None),
        P("tp", None),
        P("tp", None),
        P(),
        P(),
        P(ep, None, "tp"),
        P(ep, None, "tp"),
        P(ep, "tp", None),
        P(both, None),
    )
    out_specs = (
        P(both, None),
        P(both, None),
        P(both),
        P(ep, "tp"),
        P(ep, "tp"),
        P(ep, "tp"),
        P("tp", ep),
        P("tp", ep),
        P("tp", ep),
        P(both),
        P(both, None),
        P(ep, None, "tp"),
        P(ep, None, "tp"),
        P(ep, "tp", None),
        P(ep),
    )
    return jax.shard_map(local, mesh=cube, in_specs=in_specs, out_specs=out_specs, check_vma=False)
```

time: 577 us -> 528 us (0.915)
  matrix products: 179 us -> 81.8 us
  Pallas kernels: 0 us -> 92.8 us
  waiting for transfers between devices: 202 us -> 175 us
  local copies, waits for them, and re-layouts: 57.1 us -> 41.1 us
    pallas_call x0 -> x8, Pallas kernels: none -> 92.8 us  [the longest x1 24.6 us: expert_forward(): pl.pallas_call(expert_forward_body, grid=(steps,), in_specs=[whole] + [in...]
    dot_general x13 -> x6, matrix products: 61.6 us -> 15.5 us  [dot_rows(): lax.dot_general(left, right, (((0,), (0,)), ((), ())), preferred_element_...]
    all_gather x1, waiting for transfers between devices: 42.7 us -> 0.02 us  [local(): normed_planes = lax.all_gather(normed_own, 'z', axis=0, tiled=False)]
    dot_general x15 -> x9, matrix products: 53.5 us -> 21 us  [dot(): lax.dot_general(left, right, (((1,), (0,)), ((), ())), preferred_element_...]
    unnamed x201 -> x103, local copies, waits for them, and re-layouts: 23.3 us -> 7.49 us
    dot_general x13 -> x9, matrix products: 55.4 us -> 45.3 us  [dot_cols(): lax.dot_general(left, right, (((1,), (1,)), ((), ())), preferred_element_...]
    all_gather x1, waiting for transfers between devices: 0.01 us -> 9.75 us  [local(): mixed_planes = lax.all_gather(mixed, 'z', axis=0, tiled=False)]
    all_gather x2 -> x0, local copies, waits for them, and re-layouts: 7.98 us -> none  [the longest x1 4.04 us: local(): normed_planes = lax.all_gather(normed_own, 'z', axis=0, tiled=False)]
  transfers between devices with their start and end apart: 30 -> 30, of which waited for: 11 -> 13; matrix products, arithmetic and copies ran while one was open for 40% -> 27% of each run, Pallas kernels for 0% -> 15%
where the time goes in v2:
time: 528 us; the launch traced here: 518 us
  waiting for transfers between devices  175 us (33%)
  Pallas kernels  92.8 us (18%)
  matrix products  81.8 us (15%)
  starting transfers between devices  66.6 us (13%)
  other arithmetic  44.2 us (8%)
  local copies, waits for them, and re-layouts  41.1 us (8%)
  between operations  17 us (3%)
    all_to_all x8, waiting for transfers between devices, all_to_all(): return lax.all_to_all(value, axes, split_axis=0, concat_axis=0, tiled=True)  151 us
    all_to_all x8, starting transfers between devices, all_to_all(): return lax.all_to_all(value, axes, split_axis=0, concat_axis=0, tiled=True)  61.1 us
    dot_general x9, matrix products, dot_cols(): lax.dot_general(left, right, (((1,), (1,)), ((), ())), preferred_element_...  45.3 us
    pallas_call x1, Pallas kernels, expert_forward(): pl.pallas_call(expert_forward_body, grid=(steps,), in_specs=[whole] + [in...  24.6 us
    pallas_call x2, Pallas kernels, expert_weight_grads(): pl.pallas_call(expert_weight_grads_body, grid=(steps,), in_specs=[wide, w...  24.5 us
    dot_general x9, matrix products, dot(): lax.dot_general(left, right, (((1,), (0,)), ((), ())), preferred_element_...  21 us
    dot_general x6, matrix products, dot_rows(): lax.dot_general(left, right, (((0,), (0,)), ((), ())), preferred_element_...  15.5 us
    ppermute x20, waiting for transfers between devices, swap(): return lax.ppermute(value, 'tp', [(0, 1), (1, 0)])  14.3 us
  transfers between devices with their start and end apart: 30, of which 13 were waited for; matrix products, arithmetic and copies ran while one was open for 27% of the time, Pallas kernels for 15%

profile of v2, /device:TPU:0, one launch (start us, length us, event | category | flops | bytes accessed | tf_op | source)
XLA Modules:
  0.0 518.0 jit_solution(18191242954944297832)
XLA Ops:
  27.6 11.8 %all-to-all-start = ((bf16[64,16,2048]{2,1,0:T(8,128)(2,1)}), bf16[64,16,2048]{2,1,0:T(8,128)(2,1)}, u32[]{:S(2)}, u32[]{:S(2)}) async-start(bf16[64,16,2048]{2,1,0:T(8,128)(2,1)} %bitcast.185), calls=%async_computation | async-start | bytes 8388608 | tf_op jit(solution)/shard_map/all_to_all | solution.py:33
  41.0 8.8 %attention_forward.1 = (bf16[256,1024]{1,0:T(8,128)(2,1)}, bf16[256,1024]{1,0:T(8,128)(2,1)}, f32[8,256,256]{2,1,0:T(8,128)}, bf16[256,1024]{1,0:T(8,128)(2,1)}) custom-call(f32[256,1024]{1,0:T(8,128)} %get-tuple-element.282.refs_0_.refs_6_.query_ref, f32[256,1024]{1,0:T(8,128)} %get-tuple-element.280.refs_1_.refs_7_.key_ref, ...), custom_call_target="tpu_custom_call" | custom-call | flops 268435456 | bytes 6291456 | tf_op jit(solution)/shard_map/attention_forward/pallas_call | solution.py:108
  63.0 33.5 %all-to-all-done = bf16[64,16,2048]{2,1,0:T(8,128)(2,1)} async-done(((bf16[64,16,2048]{2,1,0:T(8,128)(2,1)}), bf16[64,16,2048]{2,1,0:T(8,128)(2,1)}, u32[]{:S(2)}, u32[]{:S(2)}) %all-to-all-start) | async-done | bytes 4194336 | tf_op jit(solution)/shard_map/all_to_all | solution.py:33
  96.5 9.5 %all-to-all-start.1 = ((bf16[64,16,2048]{2,1,0:T(8,128)(2,1)}), bf16[64,16,2048]{2,1,0:T(8,128)(2,1)}, u32[]{:S(2)}, u32[]{:S(2)}) async-start(bf16[64,16,2048]{2,1,0:T(8,128)(2,1)} %bitcast.184), calls=%async_computation.1 | async-start | bytes 8388608 | tf_op jit(solution)/shard_map/all_to_all | solution.py:33
  108.8 51.7 %all-to-all-done.1 = bf16[64,16,2048]{2,1,0:T(8,128)(2,1)} async-done(((bf16[64,16,2048]{2,1,0:T(8,128)(2,1)}), bf16[64,16,2048]{2,1,0:T(8,128)(2,1)}, u32[]{:S(2)}, u32[]{:S(2)}) %all-to-all-start.1) | async-done | bytes 4194336 | tf_op jit(solution)/shard_map/all_to_all | solution.py:33
  171.2 24.6 %expert_forward.1 = (f32[1024,512]{1,0:T(8,128)}, f32[1024,512]{1,0:T(8,128)}, f32[1024,512]{1,0:T(8,128)}, f32[1024,512]{1,0:T(8,128)}, bf16[1024,2048]{1,0:T(8,128)(2,1)}) custom-call(bf16[1024,2048]{1,0:T(8,128)(2,1)} %bitcast.19.rows_ref, bf16[2048,512]{1,0:T(8,128)(2,1)} %bitcast.229, bf16[2048,512]{1,0:T(8,128)(2,1)} %collective-permute-done.4.gate_other_ref, ...), custom_call_target="tpu_custom_call" | custom-call | flops 12884901888 | bytes 29360128 | tf_op jit(solution)/shard_map/expert_forward/pallas_call | solution.py:398
  195.8 9.8 %all-gather.7.cloned.1.call-done = bf16[1024,1024]{1,0:T(8,128)(2,1)} async-done(((bf16[256,1024]{1,0:T(8,128)(2,1)}), bf16[1024,1024]{1,0:T(8,128)(2,1)}) %all-gather.7.cloned.1.call-update) | async-done | bytes 2097168 | tf_op jit(solution)/shard_map/all_gather | solution.py:626
  205.6 9.3 %all-to-all-start.2 = ((bf16[64,16,2048]{2,1,0:T(8,128)(2,1)}), bf16[64,16,2048]{2,1,0:T(8,128)(2,1)}, u32[]{:S(2)}, u32[]{:S(2)}) async-start(bf16[64,16,2048]{2,1,0:T(8,128)(2,1)} %bitcast.188), calls=%async_computation.2 | async-start | bytes 8388608 | tf_op jit(solution)/shard_map/all_to_all | solution.py:33
  214.9 5.4 %multiply_convert_fusion.1 = (bf16[1024,512]{1,0:T(8,128)(2,1)}, bf16[1024,512]{1,0:T(8,128)(2,1)S(1)}, bf16[1024,512]{1,0:T(8,128)(2,1)S(1)}) fusion(f32[1024,512]{1,0:T(8,128)} %get-tuple-element.61, f32[1024,512]{1,0:T(8,128)} %get-tuple-element.62, f32[1024,512]{1,0:T(8,128)} %fusion.47), kind=kLoop, calls=%fused_computation.11 | loop fusion | flops 7864320 | bytes 9437184 | tf_op jit(solution)/shard_map/convert_element_type | solution.py:663
  220.3 5.7 %fusion.45 = f32[1024,2048]{1,0:T(8,128)} fusion(bf16[1024,512]{1,0:T(8,128)(2,1)S(1)} %get-tuple-element.234.gate_ref, bf16[1,2048,512]{2,1,0:T(8,128)(2,1)S(1)} %copy-done.48), kind=kOutput, calls=%fused_computation.151 | convolution fusion | flops 2147483648 | bytes 11534336 | tf_op jit(solution)/shard_map/dot_general | solution.py:29
  226.0 5.6 %fusion.43 = f32[1024,2048]{1,0:T(8,128)} fusion(bf16[1024,512]{1,0:T(8,128)(2,1)S(1)} %get-tuple-element.235.up_ref, bf16[1,2048,512]{2,1,0:T(8,128)(2,1)S(1)} %copy-done.49), kind=kOutput, calls=%fused_computation.149 | convolution fusion | flops 2147483648 | bytes 11534336 | tf_op jit(solution)/shard_map/dot_general | solution.py:29
  238.2 8.0 %fusion.67 = f32[1024,2048]{1,0:T(8,128)} fusion(bf16[1024,512]{1,0:T(8,128)(2,1)S(1)} %get-tuple-element.238.up_ref, bf16[2048,512]{1,0:T(8,128)(2,1)} %collective-permute-done.5.up_other_ref), kind=kOutput, calls=%fused_computation.173 | convolution fusion | flops 2147483648 | bytes 11534336 | tf_op jit(solution)/shard_map/dot_general | solution.py:29
  246.2 13.5 %add_convert_fusion = bf16[1024,2048]{1,0:T(8,128)(2,1)} fusion(f32[1024,2048]{1,0:T(8,128)} %fusion.67, f32[1024,2048]{1,0:T(8,128)} %fusion.45, f32[1024,2048]{1,0:T(8,128)} %fusion.43, bf16[1024,512]{1,0:T(8,128)(2,1)S(1)} %get-tuple-element.237.gate_ref, bf16[2048,512]{1,0:T(8,128)(2,1)} %collective-permute-done.4.gate_other_ref), kind=kOutput, calls=%fused_computation | convolution fusion | flops 2155872256 | bytes 32505856 | tf_op jit(solution)/shard_map/dot_general | solution.py:29
  259.7 9.3 %all-to-all-done.2 = bf16[64,16,2048]{2,1,0:T(8,128)(2,1)} async-done(((bf16[64,16,2048]{2,1,0:T(8,128)(2,1)}), bf16[64,16,2048]{2,1,0:T(8,128)(2,1)}, u32[]{:S(2)}, u32[]{:S(2)}) %all-to-all-start.2) | async-done | bytes 4194336 | tf_op jit(solution)/shard_map/all_to_all | solution.py:33
  269.0 7.4 %all-to-all-start.3 = ((bf16[64,16,2048]{2,1,0:T(8,128)(2,1)}), bf16[64,16,2048]{2,1,0:T(8,128)(2,1)}, u32[]{:S(2)}, u32[]{:S(2)}) async-start(bf16[64,16,2048]{2,1,0:T(8,128)(2,1)} %bitcast.186), calls=%async_computation.3 | async-start | bytes 8388608 | tf_op jit(solution)/shard_map/all_to_all | solution.py:33
  282.2 10.8 %expert_weight_grads.2 = (bf16[2048,512]{1,0:T(8,128)(2,1)}, bf16[2048,512]{1,0:T(8,128)(2,1)}, bf16[512,2048]{1,0:T(8,128)(2,1)}) custom-call(bf16[1024,2048]{1,0:T(8,128)(2,1)} %bitcast.19.rows_ref, bf16[1024,2048]{1,0:T(8,128)(2,1)} %copy-done.1, bf16[1024,512]{1,0:T(8,128)(2,1)} %get-tuple-element.236.inner_ref, bf16[1024,512]{1,0:T(8,128)(2,1)} %copy-done.4, ...), custom_call_target="tpu_custom_call" | custom-call | flops 100663296 | bytes 131072 | tf_op jit(solution)/shard_map/expert_weight_grads/pallas_call | solution.py:474
  302.8 26.2 %all-to-all-done.3 = bf16[64,16,2048]{2,1,0:T(8,128)(2,1)} async-done(((bf16[64,16,2048]{2,1,0:T(8,128)(2,1)}), bf16[64,16,2048]{2,1,0:T(8,128)(2,1)}, u32[]{:S(2)}, u32[]{:S(2)}) %all-to-all-start.3) | async-done | bytes 4194336 | tf_op jit(solution)/shard_map/all_to_all | solution.py:33
  353.7 13.5 %attention_backward.1 = (bf16[256,1024]{1,0:T(8,128)(2,1)}, f32[256,1024]{1,0:T(8,128)}, f32[256,1024]{1,0:T(8,128)}, f32[1,1024]{1,0:T(1,128)}, f32[1,1024]{1,0...) custom-call(bf16[256,2048]{1,0:T(8,128)(2,1)} %pad_maximum_fusion.2.refs_0_, bf16[1024,2048]{1,0:T(8,128)(2,1)} %refs_1_.1, ...), custom_call_target="tpu_custom_call" | custom-call | flops 1744830464 | bytes 14680064 | tf_op jit(solution)/shard_map/attention_backward/pallas_call | solution.py:231
  376.3 9.1 %normed_grad.1 = f32[256,2048]{1,0:T(8,128)} custom-call(bf16[256,1024]{1,0:T(8,128)(2,1)} %get-tuple-element.83.refs_0_, bf16[256,1024]{1,0:T(8,128)(2,1)} %get-tuple-element.84.refs_1_, bf16[256,1024]{1,0:T(8,128)(2,1)} %get-tuple-element.78.value_grad_ref.refs_2_, bf16[2048,1024]{1,0:T(8,128)(2,1)} %refs_3_.1, bf16[2048,1024]{1,0:T(8,128)(2,1)} %refs_4_.1, ...), custom_call_target="tpu_custom_call" | custom-call | flops 50331648 | bytes 196608 | tf_op jit(solution)/shard_map/normed_grad/pallas_call | solution.py:515
  402.6 12.2 %all-to-all-done.5 = bf16[4,256,768]{2,1,0:T(8,128)(2,1)} async-done(((bf16[4,256,768]{2,1,0:T(8,128)(2,1)}), bf16[4,256,768]{2,1,0:T(8,128)(2,1)}, u32[]{:S(2)}, u32[]{:S(2)}) %all-to-all-start.5) | async-done | bytes 1572896 | tf_op jit(solution)/shard_map/all_to_all | solution.py:33
  438.8 7.4 %weight_parcel.1 = bf16[64,208,128]{2,1,0:T(8,128)(2,1)} custom-call(bf16[1024,2048]{1,0:T(8,128)(2,1)} %bitcast.187, bf16[1024,768]{1,0:T(8,128)(2,1)} %bitcast.43.right_ref, bf16[64,16,128]{2,1,0:T(8,128)(2,1)} %concatenate.96.extra_ref), custom_call_target="tpu_custom_call" | custom-call | flops 3221225472 | bytes 9175040 | tf_op jit(solution)/shard_map/weight_parcel/pallas_call | solution.py:432
  446.2 9.0 %all-to-all-start.7 = ((bf16[64,208,128]{2,1,0:T(8,128)(2,1)}), bf16[64,208,128]{2,1,0:T(8,128)(2,1)}, u32[]{:S(2)}, u32[]{:S(2)}) async-start(bf16[64,208,128]{2,1,0:T(8,128)(2,1)} %weight_parcel.1), calls=%async_computation.7 | async-start | bytes 6815744 | tf_op jit(solution)/shard_map/all_to_all | solution.py:33
  467.0 13.7 %expert_weight_grads.3 = (f32[2048,512]{1,0:T(8,128)}, f32[2048,512]{1,0:T(8,128)}, f32[512,2048]{1,0:T(8,128)}) custom-call(bf16[1024,2048]{1,0:T(8,128)(2,1)} %bitcast.19.rows_ref, bf16[1024,2048]{1,0:T(8,128)(2,1)} %copy-done.1, bf16[1024,512]{1,0:T(8,128)(2,1)} %get-tuple-element.233.inner_ref, bf16[1024,512]{1,0:T(8,128)(2,1)} %copy-done.11, ...), custom_call_target="tpu_custom_call" | custom-call | flops 100663296 | bytes 131072 | tf_op jit(solution)/shard_map/expert_weight_grads/pallas_call | solution.py:474
  482.9 17.5 %all-to-all-done.7 = bf16[64,208,128]{2,1,0:T(8,128)(2,1)} async-done(((bf16[64,208,128]{2,1,0:T(8,128)(2,1)}), bf16[64,208,128]{2,1,0:T(8,128)(2,1)}, u32[]{:S(2)}, u32[]{:S(2)}) %all-to-all-start.7) | async-done | bytes 3407904 | tf_op jit(solution)/shard_map/all_to_all | solution.py:33
  (294 shorter events, 167.7 us)
Async XLA Ops:
  7.2 7.2 %collective-permute-start = (bf16[128,2048]{1,0:T(8,128)(2,1)}, bf16[128,2048]{1,0:T(8,128)(2,1)S(1)}, u32[]{:S(2)}, u32[]{:S(2)}) collective-permute-start(bf16[128,2048]{1,0:T(8,128)(2,1)} %param.16), channel_id=1, source_target_pairs={{0,1},{1,0},{2,3},{3,2},{4,5},{5,4},{6,7},{7,6},{8,9},{9,8},{10,11... | collective-permute-start | bytes 1572872 | tf_op jit(solution)/shard_map/ppermute | solution.py:17
  7.3 16.9 %collective-permute-start.3 = (bf16[128,2048]{1,0:T(8,128)(2,1)}, bf16[128,2048]{1,0:T(8,128)(2,1)S(1)}, u32[]{:S(2)}, u32[]{:S(2)}) collective-permute-start(bf16[128,2048]{1,0:T(8,128)(2,1)} %param.31), channel_id=1, source_target_pairs={{0,1},{1,0},{2,3},{3,2},{4,5},{5,4},{6,7},{7,6},{8,9},{9,8},{10,11... | collective-permute-start | bytes 1572872 | tf_op jit(solution)/shard_map/ppermute | solution.py:17
  22.0 17.3 %collective-permute-start.1 = (f32[2,256]{1,0:T(2,128)S(1)}, f32[2,256]{1,0:T(2,128)S(1)}, u32[]{:S(2)}, u32[]{:S(2)}) collective-permute-start(f32[2,256]{1,0:T(2,128)S(1)} %pad_maximum_fusion.6), channel_id=1, source_target_pairs={{0,1},{1,0},{2,3},{3,2},{4,5},{5,4},{6,7},{7,6},{8,9},{9,8},{10,11... | collective-permute-start | bytes 6152 | tf_op jit(solution)/shard_map/ppermute | solution.py:17
  27.6 68.9 %all-to-all-start = ((bf16[64,16,2048]{2,1,0:T(8,128)(2,1)}), bf16[64,16,2048]{2,1,0:T(8,128)(2,1)}, u32[]{:S(2)}, u32[]{:S(2)}) async-start(bf16[64,16,2048]{2,1,0:T(8,128)(2,1)} %bitcast.185), calls=%async_computation | async-start | bytes 8388608 | tf_op jit(solution)/shard_map/all_to_all | solution.py:33
  96.5 64.0 %all-to-all-start.1 = ((bf16[64,16,2048]{2,1,0:T(8,128)(2,1)}), bf16[64,16,2048]{2,1,0:T(8,128)(2,1)}, u32[]{:S(2)}, u32[]{:S(2)}) async-start(bf16[64,16,2048]{2,1,0:T(8,128)(2,1)} %bitcast.184), calls=%async_computation.1 | async-start | bytes 8388608 | tf_op jit(solution)/shard_map/all_to_all | solution.py:33
  106.1 89.8 %all-gather.5.cloned.1.call-start = ((), (), s32[]{:S(2)}) async-start(), calls=%async_computation.8 | async-start | bytes 2621440 | tf_op jit(solution)/shard_map/all_gather | solution.py:603
  108.0 97.6 %all-gather.7.cloned.1.call-start = ((), (), s32[]{:S(2)}) async-start(), calls=%async_computation.9 | async-start | bytes 2621440 | tf_op jit(solution)/shard_map/all_gather | solution.py:626
  108.1 63.1 %collective-permute-start.4 = (bf16[2048,512]{1,0:T(8,128)(2,1)}, bf16[2048,512]{1,0:T(8,128)(2,1)}, u32[]{:S(2)}, u32[]{:S(2)}) collective-permute-start(bf16[2048,512]{1,0:T(8,128)(2,1)} %bitcast.228), channel_id=1, source_target_pairs={{0,1},{1,0},{2,3},{3,2},{4,5},{5,4},{6,7},{7,6},{8,9},{9,8},{10,11... | collective-permute-start | bytes 6291464 | tf_op jit(solution)/shard_map/ppermute | solution.py:17
  108.2 63.0 %collective-permute-start.5 = (bf16[2048,512]{1,0:T(8,128)(2,1)}, bf16[2048,512]{1,0:T(8,128)(2,1)}, u32[]{:S(2)}, u32[]{:S(2)}) collective-permute-start(bf16[2048,512]{1,0:T(8,128)(2,1)} %bitcast.230), channel_id=1, source_target_pairs={{0,1},{1,0},{2,3},{3,2},{4,5},{5,4},{6,7},{7,6},{8,9},{9,8},{10,11... | collective-permute-start | bytes 6291464 | tf_op jit(solution)/shard_map/ppermute | solution.py:17
  108.7 62.5 %collective-permute-start.6 = (bf16[512,2048]{1,0:T(8,128)(2,1)}, bf16[512,2048]{1,0:T(8,128)(2,1)}, u32[]{:S(2)}, u32[]{:S(2)}) collective-permute-start(bf16[512,2048]{1,0:T(8,128)(2,1)} %bitcast.226), channel_id=1, source_target_pairs={{0,1},{1,0},{2,3},{3,2},{4,5},{5,4},{6,7},{7,6},{8,9},{9,8},{10,11... | collective-permute-start | bytes 6291464 | tf_op jit(solution)/shard_map/ppermute | solution.py:17
  205.6 63.4 %all-to-all-start.2 = ((bf16[64,16,2048]{2,1,0:T(8,128)(2,1)}), bf16[64,16,2048]{2,1,0:T(8,128)(2,1)}, u32[]{:S(2)}, u32[]{:S(2)}) async-start(bf16[64,16,2048]{2,1,0:T(8,128)(2,1)} %bitcast.188), calls=%async_computation.2 | async-start | bytes 8388608 | tf_op jit(solution)/shard_map/all_to_all | solution.py:33
  269.0 60.0 %all-to-all-start.3 = ((bf16[64,16,2048]{2,1,0:T(8,128)(2,1)}), bf16[64,16,2048]{2,1,0:T(8,128)(2,1)}, u32[]{:S(2)}, u32[]{:S(2)}) async-start(bf16[64,16,2048]{2,1,0:T(8,128)(2,1)} %bitcast.186), calls=%async_computation.3 | async-start | bytes 8388608 | tf_op jit(solution)/shard_map/all_to_all | solution.py:33
  276.4 20.9 %collective-permute-start.13 = (bf16[4,128,2048]{2,1,0:T(8,128)(2,1)}, bf16[4,128,2048]{2,1,0:T(8,128)(2,1)}, u32[]{:S(2)}, u32[]{:S(2)}) collective-permute-start(bf16[4,128,2048]{2,1,0:T(8,128)(2,1)} %bitcast.190), channel_id=1, source_target_pairs={{0,1},{1,0},{2,3},{3,2},{4,5},{5,4},{6,7},{7,6},{8,9},{9,8},{10,11... | collective-permute-start | bytes 6291464 | tf_op jit(solution)/shard_map/ppermute | solution.py:17
  332.7 8.5 %collective-permute-start.8 = (f32[128,2048]{1,0:T(8,128)S(1)}, f32[128,2048]{1,0:T(8,128)S(1)}, u32[]{:S(2)}, u32[]{:S(2)}) collective-permute-start(f32[128,2048]{1,0:T(8,128)S(1)} %slice.266), channel_id=1, source_target_pairs={{0,1},{1,0},{2,3},{3,2},{4,5},{5,4},{6,7},{7,6},{8,9},{9,8},{10,11... | collective-permute-start | bytes 3145736 | tf_op jit(solution)/shard_map/ppermute | solution.py:17
  344.6 7.0 %collective-permute-start.10 = (bf16[128,2048]{1,0:T(8,128)(2,1)}, bf16[128,2048]{1,0:T(8,128)(2,1)S(1)}, u32[]{:S(2)}, u32[]{:S(2)}) collective-permute-start(bf16[128,2048]{1,0:T(8,128)(2,1)} %get-tuple-element.227), channel_id=1, source_target_pairs={{0,1},{1,0},{2,3},{3,2},{4,5},{5,4},{6,7},{7,6},{8,9},{9,8},{10,11... | collective-permute-start | bytes 1572872 | tf_op jit(solution)/shard_map/ppermute | solution.py:17
  347.0 20.2 %all-to-all-start.4 = ((bf16[4,128,512]{2,1,0:T(8,128)(2,1)}), bf16[4,128,512]{2,1,0:T(8,128)(2,1)}, u32[]{:S(2)}, u32[]{:S(2)}) async-start(bf16[4,128,512]{2,1,0:T(8,128)(2,1)} %pad_maximum_fusion.3), calls=%async_computation.4 | async-start | bytes 1048576 | tf_op jit(solution)/shard_map/all_to_all | solution.py:33
  387.7 11.6 %collective-permute-start.12 = (f32[128,2048]{1,0:T(8,128)}, f32[128,2048]{1,0:T(8,128)S(1)}, u32[]{:S(2)}, u32[]{:S(2)}) collective-permute-start(f32[128,2048]{1,0:T(8,128)} %slice.280), channel_id=1, source_target_pairs={{0,1},{1,0},{2,3},{3,2},{4,5},{5,4},{6,7},{7,6},{8,9},{9,8},{10,11... | collective-permute-start | bytes 3145736 | tf_op jit(solution)/shard_map/ppermute | solution.py:17
  388.4 6.6 %collective-permute-start.14 = (bf16[4,128,512]{2,1,0:T(8,128)(2,1)}, bf16[4,128,512]{2,1,0:T(8,128)(2,1)}, u32[]{:S(2)}, u32[]{:S(2)}) collective-permute-start(bf16[4,128,512]{2,1,0:T(8,128)(2,1)} %all-to-all-done.4), channel_id=1, source_target_pairs={{0,1},{1,0},{2,3},{3,2},{4,5},{5,4},{6,7},{7,6},{8,9},{9,8},{10,11... | collective-permute-start | bytes 1572872 | tf_op jit(solution)/shard_map/ppermute | solution.py:17
  388.7 26.1 %all-to-all-start.5 = ((bf16[4,256,768]{2,1,0:T(8,128)(2,1)}), bf16[4,256,768]{2,1,0:T(8,128)(2,1)}, u32[]{:S(2)}, u32[]{:S(2)}) async-start(bf16[4,256,768]{2,1,0:T(8,128)(2,1)} %get-tuple-element.88), calls=%async_computation.5 | async-start | bytes 3145728 | tf_op jit(solution)/shard_map/all_to_all | solution.py:33
  414.8 31.4 %all-to-all-start.6 = ((bf16[16,32,1024]{2,1,0:T(8,128)(2,1)}), bf16[16,32,1024]{2,1,0:T(8,128)(2,1)S(1)}, u32[]{:S(2)}, u32[]{:S(2)}) async-start(bf16[16,32,1024]{2,1,0:T(8,128)(2,1)} %bitcast.192), calls=%async_computation.6 | async-start | bytes 2097152 | tf_op jit(solution)/shard_map/all_to_all | solution.py:33
  421.1 10.8 %collective-permute-start.16 = (f32[64,16]{1,0:T(8,128)}, f32[64,16]{1,0:T(8,128)}, u32[]{:S(2)}, u32[]{:S(2)}) collective-permute-start(f32[64,16]{1,0:T(8,128)} %select_bitcast_fusion), channel_id=1, source_target_pairs={{0,1},{1,0},{2,3},{3,2},{4,5},{5,4},{6,7},{7,6},{8,9},{9,8},{10,11... | collective-permute-start | bytes 12296 | tf_op jit(solution)/shard_map/ppermute | solution.py:17
  446.2 54.1 %all-to-all-start.7 = ((bf16[64,208,128]{2,1,0:T(8,128)(2,1)}), bf16[64,208,128]{2,1,0:T(8,128)(2,1)}, u32[]{:S(2)}, u32[]{:S(2)}) async-start(bf16[64,208,128]{2,1,0:T(8,128)(2,1)} %weight_parcel.1), calls=%async_computation.7 | async-start | bytes 6815744 | tf_op jit(solution)/shard_map/all_to_all | solution.py:33
  455.5 7.1 %collective-permute-start.18 = (bf16[2048,512]{1,0:T(8,128)(2,1)}, bf16[2048,512]{1,0:T(8,128)(2,1)S(1)}, u32[]{:S(2)}, u32[]{:S(2)}) collective-permute-start(bf16[2048,512]{1,0:T(8,128)(2,1)} %get-tuple-element.96), channel_id=1, source_target_pairs={{0,1},{1,0},{2,3},{3,2},{4,5},{5,4},{6,7},{7,6},{8,9},{9,8},{10,11... | collective-permute-start | bytes 6291464 | tf_op jit(solution)/shard_map/ppermute | solution.py:17
  455.8 9.9 %collective-permute-start.19 = (bf16[512,2048]{1,0:T(8,128)(2,1)}, bf16[512,2048]{1,0:T(8,128)(2,1)S(1)}, u32[]{:S(2)}, u32[]{:S(2)}) collective-permute-start(bf16[512,2048]{1,0:T(8,128)(2,1)} %get-tuple-element.97), channel_id=1, source_target_pairs={{0,1},{1,0},{2,3},{3,2},{4,5},{5,4},{6,7},{7,6},{8,9},{9,8},{10,11... | collective-permute-start | bytes 6291464 | tf_op jit(solution)/shard_map/ppermute | solution.py:17
  (56 other events, 769.1 us)
Sparse Core Ops, SparseCore 0:
  108.6 64.5 all-gather.4
  175.4 30.1 all-gather.6
